TPU v7x, 128 devices: a whole 4x4x4 slice. The times are simulated.
128 devices in a mesh: tm: 16 (over y, x), space: 8 (over z, core).
Axes of the slice: x: 4, y: 4, z: 4, core: 2. Of those that a mesh axis runs over, the one named last changes fastest.
Arguments:
- queries: bfloat16 [32, 32, 16, 1024], P('tm', None, 'space'), may hold values from -16 to 16
- key_rows: bfloat16 [32, 32, 16, 1024], P('tm', None, 'space'), may hold values from -6 to 6
- value_rows: bfloat16 [32, 32, 16, 1024], P('tm', None, 'space'), may hold values from -5 to 5
- out_proj: bfloat16 [1024, 512], replicated, may hold values from -0.1875 to 0.1875
- conv_taps: bfloat16 [3, 3, 3, 512, 512], replicated, may hold values from -0.0546875 to 0.0546875
- cotangent: bfloat16 [32, 32, 16, 512], P('tm', None, 'space'), may hold values from -6 to 6
Outputs:
- conv_output: bfloat16 [32, 32, 16, 512], P('tm', None, 'space')
- grad_queries: bfloat16 [32, 32, 16, 1024], P('tm', None, 'space')
- grad_keys: bfloat16 [32, 32, 16, 1024], P('tm', None, 'space')
- grad_values: bfloat16 [32, 32, 16, 1024], P('tm', None, 'space')
All inputs are finite; a program needn't handle non-finite values.
Results may differ from a plain program's by a relative error of at most 0.019.
Values may be sent and summed in bfloat16 or wider, within the bound.
No kernel may reach another device: no remote copies, remote signals or barrier semaphores. Data moves between devices by JAX's collectives and lax.ppermute only.
A program may use at most 128 MiB of HBM per device.

v0:
```python
import functools

import jax
import jax.numpy as jnp
from jax import lax
from jax.experimental import pallas as pl
from jax.experimental.pallas import tpu as pltpu
from jax.sharding import Mesh, PartitionSpec as P


HEAD = 64
NEGATIVE = -1e30
BF = jnp.bfloat16
F32 = jnp.float32
NN = (((1,), (0,)), ((), ()))
NT = (((1,), (1,)), ((), ()))
AXES = ("y", "x", "z", "c")
ROWS = 32
TOK = 512
SPAN = 4 * TOK
LIMIT = 60 * 2**20


def dot(a, b, dims=NN):
    return lax.dot_general(a, b, dims, preferred_element_type=F32)


def kernel_call(body, outs, scratch, args, grid=(1,), specs=None, us=1.0):
    def whole(shape):
        rank = len(shape)
        return pl.BlockSpec(shape, lambda *_: (0,) * rank)

    in_specs = [whole(a.shape) for a in args]
    for index, spec in (specs or {}).items():
        in_specs[index] = spec
    return pl.pallas_call(
        body,
        out_shape=outs,
        grid=grid,
        in_specs=in_specs,
        out_specs=[whole(o.shape) for o in outs],
        scratch_shapes=scratch,
        compiler_params=pltpu.CompilerParams(vmem_limit_bytes=LIMIT),
        cost_estimate=pl.CostEstimate(
            flops=int(us * 8e8), bytes_accessed=int(us * 1e6), transcendentals=0
        ),
    )(*args)


def struct(shape, dtype=BF):
    return jax.ShapeDtypeStruct(shape, dtype)


def write_rows(value, head, place, out_ref, stage_ref):
    for frame in range(2):
        stage_ref[head, pl.ds(frame, ROWS, stride=2), :] = value[frame * ROWS : (frame + 1) * ROWS]
    out_ref[:, head, :, place] = stage_ref[head].reshape(4, 2, 8, 128).astype(BF)


def write_columns(tile_of, out_ref, stage_ref, place):
    lane = lax.broadcasted_iota(jnp.int32, (1, 128), 1)
    for tile in range(8):
        value = tile_of(tile)
        first = value[: 2 * ROWS]
        second = value[2 * ROWS :]
        even = jnp.where(lane < HEAD, first, pltpu.roll(second, HEAD, 1))
        odd = jnp.where(lane < HEAD, pltpu.roll(first, HEAD, 1), second)
        write_rows(even, 2 * tile, place, out_ref, stage_ref)
        write_rows(odd, 2 * tile + 1, place, out_ref, stage_ref)


def write_pairs(low, high, out_ref, stage_ref, place):
    lane = lax.broadcasted_iota(jnp.int32, (1, 128), 1)
    for tile in range(8):
        a = low(tile)
        b = high(tile)
        even = jnp.where(lane < HEAD, a, pltpu.roll(b, HEAD, 1))
        odd = jnp.where(lane < HEAD, pltpu.roll(a, HEAD, 1), b)
        for half, value in ((0, even), (1, odd)):
            for col in range(2):
                part = value[col * 2 * ROWS : (col + 1) * 2 * ROWS]
                write_rows(part, 2 * tile + half, place + col, out_ref, stage_ref)


def read_rows(value, slot, col, tile, target, stage_ref):
    stage_ref[slot] = value
    for frame in range(2):
        row = (col * 2 + frame) * ROWS
        target[row : row + ROWS, tile * 128 : (tile + 1) * 128] = stage_ref[
            slot, pl.ds(frame, ROWS, stride=2), :
        ].astype(BF)


def heads_of(in_ref, tile, place):
    even = in_ref[:, 2 * tile, :, place].astype(F32).reshape(2 * ROWS, 128)
    odd = in_ref[:, 2 * tile + 1, :, place].astype(F32).reshape(2 * ROWS, 128)
    lane = lax.broadcasted_iota(jnp.int32, (1, 128), 1)
    low = jnp.where(lane < HEAD, even, pltpu.roll(odd, HEAD, 1))
    high = jnp.where(lane < HEAD, pltpu.roll(even, HEAD, 1), odd)
    return low, high


def read_columns(in_ref, target, stage_ref, place):
    for tile in range(8):
        low, high = heads_of(in_ref, tile, place)
        read_rows(low, 2 * tile, 0, tile, target, stage_ref)
        read_rows(high, 2 * tile + 1, 1, tile, target, stage_ref)


def read_pairs(in_ref, low_ref, high_ref, stage_ref, place):
    for tile in range(8):
        for col in range(2):
            low, high = heads_of(in_ref, tile, place + col)
            read_rows(low, 2 * tile, col, tile, low_ref, stage_ref)
            read_rows(high, 2 * tile + 1, col, tile, high_ref, stage_ref)


def tiles_of(ref):
    return lambda tile: ref[:, tile * 128 : (tile + 1) * 128].astype(F32)


def pack_body(q_ref, k_ref, v_ref, out_ref, stage_ref):
    write_columns(tiles_of(q_ref), out_ref, stage_ref, 0)
    write_pairs(tiles_of(k_ref), tiles_of(v_ref), out_ref, stage_ref, 1)


def extend(own_ref, near_ref, ext_ref, reverse):
    row = lax.broadcasted_iota(jnp.int32, (2 * ROWS, 1), 0) % ROWS
    for part, ref in enumerate((own_ref, near_ref)):
        first = 2 * part if reverse else 2 - 2 * part
        for col in range(4):
            value = ref[col].astype(F32).reshape(2 * ROWS, -1)
            up = jnp.where(row == 0, 0.0, pltpu.roll(value, 1, 0))
            down = jnp.where(row == ROWS - 1, 0.0, pltpu.roll(value, 2 * ROWS - 1, 0))
            for shift, moved in enumerate((up, value, down)):
                ext_ref[shift, col, first : first + 2] = moved.astype(BF).reshape(2, ROWS, -1)


def conv_step(own_ref, near_ref, taps_ref, ext_ref, acc_ref, reverse):
    step = pl.program_id(0)
    lag = step // 3
    shift = step % 3

    @pl.when(step == 0)
    def _():
        extend(own_ref, near_ref, ext_ref, reverse)
        acc_ref[...] = own_ref[1:3].astype(F32).reshape(4 * ROWS, -1)

    if reverse:
        lag = 2 - lag
        shift = 2 - shift
    total = None
    for b in range(3):
        col = 2 - b if reverse else b
        window = ext_ref[shift, col : col + 2, pl.ds(lag, 2)].reshape(4 * ROWS, -1)
        part = dot(window, taps_ref[0, 0, b], NT if reverse else NN)
        total = part if total is None else total + part
    acc_ref[...] += total


def conv_body(own_ref, near_ref, taps_ref, out_ref, ext_ref, acc_ref):
    conv_step(own_ref, near_ref, taps_ref, ext_ref, acc_ref, False)

    @pl.when(pl.program_id(0) == 8)
    def _():
        out_ref[...] = acc_ref[...].astype(BF)


def adjoint_body(own_ref, near_ref, taps_ref, proj_ref, out_ref, ext_ref, acc_ref, stage_ref):
    conv_step(own_ref, near_ref, taps_ref, ext_ref, acc_ref, True)

    @pl.when(pl.program_id(0) == 8)
    def _():
        grad = acc_ref[...].astype(BF)

        def tile_of(tile):
            return dot(grad, proj_ref[tile * 128 : (tile + 1) * 128, :], NT)

        write_columns(tile_of, out_ref, stage_ref, 0)


def project_body(in_ref, proj_ref, out_ref, att_ref, stage_ref):
    read_columns(in_ref, att_ref, stage_ref, 0)
    out_ref[...] = dot(att_ref[...], proj_ref[...]).astype(BF)


def unpack_body(in_ref, gq_ref, gk_ref, gv_ref, stage_ref):
    read_columns(in_ref, gq_ref, stage_ref, 0)
    read_pairs(in_ref, gk_ref, gv_ref, stage_ref, 1)


def join_columns(value, out_ref, base, roll_low):
    lane = lax.broadcasted_iota(jnp.int32, (1, 128), 1)
    for x in range(4):
        first = value[x * 128 : x * 128 + 64]
        second = value[x * 128 + 64 : (x + 1) * 128]
        if roll_low:
            first = pltpu.roll(first, HEAD, 1)
        else:
            second = pltpu.roll(second, HEAD, 1)
        out_ref[pl.ds(pl.multiple_of(base + x * 64, 64), 64), :] = jnp.where(
            lane < HEAD, first, second
        ).astype(BF)


def split_columns(value, out_ref, group, high):
    lane = lax.broadcasted_iota(jnp.int32, (1, 128), 1)
    keep = lane >= HEAD if high else lane < HEAD
    moved = pltpu.roll(value, HEAD, 1)
    first, second = (moved, value) if high else (value, moved)
    out_ref[group * 128 : group * 128 + 64, :] = jnp.where(keep, first, 0.0).astype(BF)
    out_ref[group * 128 + 64 : (group + 1) * 128, :] = jnp.where(keep, second, 0.0).astype(BF)


def forward_body(number, first, last, *refs):
    refs = list(refs)
    kv_refs = [refs.pop(0) for _ in range(number)]
    source_ref = refs.pop(0)
    if not first:
        seed_ref = refs.pop(0)
    if last:
        do_ref = refs.pop(0)
        att_ref, stat_ref, grad_ref, kv_ref, max_ref, acc_ref, sems = refs
        query_ref = source_ref
    elif first:
        query_ref, state_ref, kv_ref, max_ref, acc_ref, sems = refs
    else:
        state_ref, kv_ref, max_ref, acc_ref, sems = refs
        query_ref = source_ref
    lane = lax.broadcasted_iota(jnp.int32, (1, 128), 1)
    one = jnp.ones((), BF)
    copies = [
        pltpu.make_async_copy(kv_refs[i], kv_ref.at[:, :, i], sems.at[i]) for i in range(number)
    ]
    for copy in copies:
        copy.start()
    for group in range(16):
        rows = slice(group * 8, (group + 1) * 8)
        if first:
            value = source_ref[rows].astype(F32).reshape(64, 128) * HEAD**-0.5
            split_columns(value, query_ref, group, False)
        if last:
            split_columns(do_ref[rows].astype(F32).reshape(64, 128), grad_ref, group, True)
    for copy in copies:
        copy.wait()

    def per_block(block, _):
        start = block * TOK
        rows = pl.ds(pl.multiple_of(start, TOK), TOK)
        if first:
            max_ref[...] = jnp.full(max_ref.shape, NEGATIVE, F32)
            acc_ref[...] = jnp.zeros(acc_ref.shape, F32)
        else:
            max_ref[...] = jnp.broadcast_to(seed_ref[rows, 1:2], max_ref.shape)
            acc_ref[...] = seed_ref[rows, :]

        def update(part, scores, keys):
            before = max_ref[part, :]
            high = jnp.max(scores, axis=1, keepdims=True)
            after = jnp.maximum(before, jnp.broadcast_to(high, before.shape))
            shift = jnp.concatenate([after] * (scores.shape[1] // 128), axis=1)
            weights = jnp.exp(scores - shift).astype(BF)
            moved = dot(weights, jnp.where(lane < HEAD, one, keys))
            acc_ref[part, :] = acc_ref[part, :] * jnp.exp(before - after) + moved
            max_ref[part, :] = after

        def whole(index, _):
            keys = kv_ref[index].reshape(number * TOK, 128)
            update(slice(None), dot(query_ref[rows, :], keys, NT), keys)
            return 0

        lax.fori_loop(0, block, whole, 0)
        for half in range(2):
            count = TOK - 256 * half
            query = query_ref[pl.ds(pl.multiple_of(start + half * 256, 256), count), :]
            keys = kv_ref[block, 2 * half : 2 * half + 2].reshape(number * 256, 128)
            row = lax.broadcasted_iota(jnp.int32, (count, 1), 0)
            key = lax.broadcasted_iota(jnp.int32, (1, number * 256), 1)
            hidden = row // 128 * 2 + row % 2 < key // (number * 128) * 2 + key % 2
            scores = jnp.where(hidden, NEGATIVE, dot(query, keys, NT))
            update(slice(half * 256, TOK), scores, keys)
        acc = acc_ref[...]
        if not last:
            state_ref[rows, :] = jnp.where(lane == 1, max_ref[...], acc)
            return 0
        total = acc[:, 0:1]
        att = (acc / total).astype(BF).astype(F32)
        delta = jnp.sum(att * grad_ref[rows, :].astype(F32), axis=1, keepdims=True)
        logsum = max_ref[:, 0:1] + jnp.log(total)
        stat_ref[:, rows] = jnp.where(lane == 0, logsum, delta).T[0:8, :]
        join_columns(att, att_ref, block * 256, True)
        return 0

    lax.fori_loop(0, 4, per_block, 0)


def backward_body(first, last, same_ref, other_ref, query_ref, grad_ref, stat_ref, *refs):
    refs = list(refs)
    seed_ref = None if first else refs.pop(0)
    same_out, other_out, dq_out, kv_ref, turned_ref, acc_ref, dq_ref = refs
    eye = (
        lax.broadcasted_iota(jnp.int32, (128, 128), 0)
        == lax.broadcasted_iota(jnp.int32, (128, 128), 1)
    ).astype(BF)
    kv_ref[:, :, 0] = same_ref[...]
    kv_ref[:, :, 1] = other_ref[...]
    dq_ref[...] = jnp.zeros(dq_ref.shape, F32) if first else seed_ref[...]

    def per_keys(block, _):
        turned_ref[...] = dot(eye, kv_ref[block].reshape(2 * TOK, 128), NT).astype(BF)
        acc_ref[...] = jnp.zeros(acc_ref.shape, F32)

        def pairs(start, count, part, masked):
            rows = pl.ds(pl.multiple_of(start, 128), count)
            query = query_ref[rows, :]
            grad = grad_ref[rows, :]
            stats = stat_ref[:, rows]
            keys = kv_ref[block].reshape(2 * TOK, 128)[part]
            probs = jnp.exp(dot(keys, query, NT) - stats[0:1, :])
            if masked:
                key = lax.broadcasted_iota(jnp.int32, (keys.shape[0], 1), 0)
                row = lax.broadcasted_iota(jnp.int32, (1, count), 1)
                hidden = key // 256 * 2 + key % 2 > row // 128 * 2 + row % 2
                probs = jnp.where(hidden, 0.0, probs)
            inner = (probs * (dot(keys, grad, NT) - stats[1:2, :])).astype(BF)
            acc_ref[part, :] += dot(inner, query) + dot(probs.astype(BF), grad)
            dq_ref[:, rows] += dot(turned_ref[:, part], inner)

        def whole(later, _):
            pairs(later * TOK, TOK, slice(0, 2 * TOK), False)
            return 0

        lax.fori_loop(block + 1, 4, whole, 0)
        pairs(block * TOK, TOK, slice(0, TOK), True)
        pairs(block * TOK + 256, 256, slice(TOK, 2 * TOK), True)
        total = acc_ref[...].astype(BF).reshape(4, 2, 128, 128)
        same_out[block] = total[:, 0]
        other_out[block] = total[:, 1]
        return 0

    lax.fori_loop(0, 4, per_keys, 0)
    if last:
        for block in range(4):
            value = (dq_ref[:, block * TOK : (block + 1) * TOK] * HEAD**-0.5).T
            join_columns(value, dq_out, block * 256, False)
    else:
        dq_out[...] = dq_ref[...]


def shift_y(value, steps):
    return lax.ppermute(value, "y", [(i, (i + steps) % 4) for i in range(4)])


def swap_core(value):
    return lax.ppermute(value, "c", [(0, 1), (1, 0)])


def halo(own, forward):
    step = 1 if forward else -1

    def turn(value, cols):
        pairs = [(i, (i + cols) % 8) for i in range(8)]
        return lax.ppermute(value, ("z", "c"), pairs)

    left = turn(own[1:], 1)
    right = turn(own[:1], -1)
    wide = jnp.concatenate([left, own, right], axis=0)
    frames = [(t, t + step) for t in range(16) if 0 <= t + step < 16]
    return wide, lax.ppermute(wide, ("y", "x"), frames)


def exchange_all(value):
    split = value.reshape(128, -1, 128)
    return lax.all_to_all(split, AXES, split_axis=0, concat_axis=0, tiled=True)


def columns_first(array):
    return array.transpose(2, 0, 1, 3)


def flat(array):
    return columns_first(array).reshape(4 * ROWS, -1)


def tokens_back(array):
    return array.reshape(2, 2, ROWS, -1).transpose(1, 2, 0, 3)


def shards(queries, key_rows, value_rows, out_proj, conv_taps, cotangent):
    channels = out_proj.shape[1]
    stage = pltpu.VMEM((16, 2 * ROWS, 128), F32)
    taps_spec = pl.BlockSpec((1, 1, 3, channels, channels), lambda t: (t // 3, t % 3, 0, 0, 0))
    conv_scratch = [
        pltpu.VMEM((3, 4, 4, ROWS, channels), BF),
        pltpu.VMEM((4 * ROWS, channels), F32),
    ]
    grouped = (4, 4, 128, 128)

    near = halo(columns_first(cotangent), False)
    (packed,) = kernel_call(
        pack_body,
        [struct((4, 16, 2, 3, 8, 128))],
        [stage],
        (flat(queries), flat(key_rows), flat(value_rows)),
        us=4.0,
    )
    packed = exchange_all(packed)
    (grad,) = kernel_call(
        adjoint_body,
        [struct((4, 16, 2, 1, 8, 128))],
        [*conv_scratch, stage],
        (*near, conv_taps, out_proj),
        grid=(9,),
        specs={2: taps_spec},
        us=12.0,
    )
    packed, grad = lax.optimization_barrier((packed, grad))
    source = packed[:, :8]
    kv_same = {0: packed[:, 8:].reshape(grouped)}
    for steps in (1, 3, 2):
        kv_same[steps] = shift_y(kv_same[0], steps)
    kv_other = {steps: swap_core(kv_same[steps]) for steps in (0, 1, 3, 2)}
    grad = exchange_all(grad)

    def attend(arrays, extra, outs, us, first=False, last=False):
        number = len(arrays)
        return kernel_call(
            functools.partial(forward_body, number, first, last),
            outs,
            [
                pltpu.VMEM((4, 4, number, 128, 128), BF),
                pltpu.VMEM((TOK, 128), F32),
                pltpu.VMEM((TOK, 128), F32),
                pltpu.SemaphoreType.DMA((number,)),
            ],
            (*arrays, *extra),
            specs={index: pl.BlockSpec(memory_space=pl.ANY) for index in range(number)},
            us=us,
        )

    state = struct((SPAN, 128), F32)
    query, seed = attend(
        [kv_same[0], kv_other[0]], (source,), [struct((SPAN, 128)), state], 10.0, True
    )
    (seed,) = attend([kv_same[i] for i in (1, 3, 2)], (query, seed), [state], 15.0)
    att, stats, grad = attend(
        [kv_other[i] for i in (1, 3, 2)],
        (query, seed, grad),
        [struct((SPAN // 2, 128)), struct((8, SPAN), F32), struct((SPAN, 128))],
        15.0,
        last=True,
    )
    att = exchange_all(att).reshape(4, 16, 2, 1, 8, 128)

    seed = None
    total = None
    for steps in (2, 1, 3, 0):
        last = steps == 0
        same, other, seed = kernel_call(
            functools.partial(backward_body, seed is None, last),
            [
                struct(grouped),
                struct(grouped),
                struct((SPAN // 2, 128)) if last else struct((128, SPAN), F32),
            ],
            [
                pltpu.VMEM((4, 4, 2, 128, 128), BF),
                pltpu.VMEM((128, 2 * TOK), BF),
                pltpu.VMEM((2 * TOK, 128), F32),
                pltpu.VMEM((128, SPAN), F32),
            ],
            (kv_same[steps], kv_other[steps], query, grad, stats)
            + (() if seed is None else (seed,)),
            us=16.0,
        )
        joined = same.astype(F32) + swap_core(other).astype(F32)
        if not last:
            joined = shift_y(joined.astype(BF), 4 - steps).astype(F32)
        total = joined if total is None else total + joined
    (projected,) = kernel_call(
        project_body,
        [struct((4 * ROWS, channels))],
        [pltpu.VMEM((4 * ROWS, 1024), BF), stage],
        (att, out_proj),
        us=3.0,
    )
    near = halo(projected.reshape(2, 2, ROWS, channels), True)
    (conv,) = kernel_call(
        conv_body,
        [struct((4 * ROWS, channels))],
        conv_scratch,
        (*near, conv_taps),
        grid=(9,),
        specs={2: taps_spec},
        us=10.0,
    )
    grads = jnp.concatenate(
        [seed.reshape(128, 8, 128), total.astype(BF).reshape(128, 16, 128)], axis=1
    )
    grads = exchange_all(grads).reshape(4, 16, 2, 3, 8, 128)
    grads = kernel_call(unpack_body, [struct((4 * ROWS, 1024))] * 3, [stage], (grads,), us=4.0)
    return (tokens_back(conv), *(tokens_back(g) for g in grads))


def solution(mesh):
    grid = Mesh(mesh.devices.reshape(4, 4, 4, 2), AXES)
    spec = P(("y", "x"), None, ("z", "c"), None)
    return jax.shard_map(
        shards,
        mesh=grid,
        in_specs=(spec, spec, spec, P(), P(), spec),
        out_specs=(spec,) * 4,
        check_vma=False,
    )
```

profile of v0, /device:TPU:1, one launch (start us, length us, event | category | flops | bytes accessed | tf_op | source)
XLA Modules:
  0.0 261.6 jit_solution(198519181421222980)
XLA Ops:
  1.6 3.0 %collective-permute-start = (bf16[1,2,32,512]{3,2,1,0:T(8,128)(2,1)S(1)}, bf16[1,2,32,512]{3,2,1,0:T(8,128)(2,1)S(1)}, u32[]{:S(2)}, u32[]{:S(2)}) collective-permute-start(bf16[1,2,32,512]{3,2,1,0:T(8,128)(2,1)S(1)} %get-tuple-element.50), channel_id=1, source_target_pairs={{0,1},{1,2},{2,3},{3,4},{4,5},{5,6},{6,7},{7,0},{8,9},{9,10},{10,1... | collective-permute-start | bytes 196616 | tf_op jit(solution)/shard_map/ppermute | solution.py:363
  4.7 1.7 copy.10
  6.4 1.7 copy.11
  10.2 2.4 shard_map.93
  12.6 11.4 %all-to-all-start = ((bf16[128,24,128]{2,1,0:T(8,128)(2,1)}), bf16[128,24,128]{2,1,0:T(8,128)(2,1)S(1)}, u32[]{:S(2)}, u32[]{:S(2)}) async-start(bf16[128,24,128]{2,1,0:T(8,128)(2,1)} %bitcast.38), calls=%async_computation | async-start | bytes 1572864 | tf_op jit(solution)/shard_map/all_to_all | solution.py:374
  24.7 12.4 %shard_map.94 = bf16[4,16,2,1,8,128]{5,4,3,2,1,0:T(8,128)(2,1)} custom-call(bf16[4,2,32,512]{3,2,1,0:T(8,128)(2,1)} %copy-done.10, bf16[4,2,32,512]{3,2,1,0:T(8,128)(2,1)} %copy-done.16, bf16[3,3,3,512,512]{4,3,2,1,0:T(8,128)(2,1)} %taps_ref.3, bf16[1024,512]{1,0:T(8,128)(2,1)} %proj_ref.3), custom_call_target="tpu_custom_call" | custom-call | flops 9600000000 | bytes 12000000 | tf_op jit(solution)/shard_map/pallas_call | solution.py:36
  37.2 3.1 %all-to-all-done = bf16[128,24,128]{2,1,0:T(8,128)(2,1)S(1)} async-done(((bf16[128,24,128]{2,1,0:T(8,128)(2,1)}), bf16[128,24,128]{2,1,0:T(8,128)(2,1)S(1)}, u32[]{:S(2)}, u32[]{:S(2)}) %all-to-all-start) | async-done | bytes 786464 | tf_op jit(solution)/shard_map/all_to_all | solution.py:374
  40.7 2.3 collective-permute-start.5
  43.0 1.9 collective-permute-start.9
  45.6 5.9 %all-to-all-start.1 = ((bf16[128,8,128]{2,1,0:T(8,128)(2,1)}), bf16[128,8,128]{2,1,0:T(8,128)(2,1)S(1)}, u32[]{:S(2)}, u32[]{:S(2)}) async-start(bf16[128,8,128]{2,1,0:T(8,128)(2,1)} %bitcast.9), calls=%async_computation.1 | async-start | bytes 524288 | tf_op jit(solution)/shard_map/all_to_all | solution.py:374
  51.5 2.9 %collective-permute-done.3.refs_0_.same_ref = bf16[4,4,128,128]{3,2,1,0:T(8,128)(2,1)S(1)} collective-permute-done((bf16[4,4,128,128]{3,2,1,0:T(8,128)(2,1)S(1)}, bf16[4,4,128,128]{3,2,1,0:T(8,128)(2,1)S(1)}, u32[]{:S(2)}, u32[]{:S(2)}) %collective-permute-start.3) | collective-permute-done | bytes 524320 | tf_op jit(solution)/shard_map/ppermute | solution.py:351
  54.5 15.3 %collective-permute-start.4 = (bf16[4,4,128,128]{3,2,1,0:T(8,128)(2,1)S(1)}, bf16[4,4,128,128]{3,2,1,0:T(8,128)(2,1)}, u32[]{:S(2)}, u32[]{:S(2)}) collective-permute-start(bf16[4,4,128,128]{3,2,1,0:T(8,128)(2,1)S(1)} %collective-permute-done.3.refs_0_.same_ref), channel_id=1, source_target_pairs={{0,1},{1,0},{2,3},{3,2},{4,5},{5,4},{6,7},{7,6},{8,9},{9,8},{10,11... | collective-permute-start | bytes 1572872 | tf_op jit(solution)/shard_map/ppermute | solution.py:355
  71.1 12.0 %shard_map.95 = (bf16[2048,128]{1,0:T(8,128)(2,1)}, f32[2048,128]{1,0:T(8,128)}) custom-call(bf16[4,4,128,128]{3,2,1,0:T(8,128)(2,1)} %bitcast.43, bf16[4,4,128,128]{3,2,1,0:T(8,128)(2,1)} %copy-done.12, bf16[128,8,128]{2,1,0:T(8,128)(2,1)} %slice.27.refs_2_), custom_call_target="tpu_custom_call" | custom-call | flops 8000000000 | bytes 10000000 | tf_op jit(solution)/shard_map/pallas_call | solution.py:36
  83.1 16.2 %shard_map.96.refs_4_ = f32[2048,128]{1,0:T(8,128)} custom-call(bf16[4,4,128,128]{3,2,1,0:T(8,128)(2,1)} %copy-done.14, bf16[4,4,128,128]{3,2,1,0:T(8,128)(2,1)} %copy-done.13, bf16[4,4,128,128]{3,2,1,0:T(8,128)(2,1)} %collective-permute-done.7.refs_2_.same_ref, bf16[2048,128]{1,0:T(8,128)(2,1)} %get-tuple-element.27.refs_3_.query_ref, ...), custom_call_target="tpu_custom_call" | custom-call | flops 12000000000 | bytes 15000000 | tf_op jit(solution)/shard_map/pallas_call | solution.py:36
  100.3 17.5 %shard_map.97 = (bf16[1024,128]{1,0:T(8,128)(2,1)}, f32[8,2048]{1,0:T(8,128)}, bf16[2048,128]{1,0:T(8,128)(2,1)}) custom-call(bf16[4,4,128,128]{3,2,1,0:T(8,128)(2,1)} %collective-permute-done.4.refs_0_.other_ref, bf16[4,4,128,128]{3,2,1,0:T(8,128)(2,1)} %copy-done.15, bf16[4,4,128,128]{3,2,1,0:T(8,128)(2,1)} %collective-permute-done.8.refs_2_.other_ref, ...), custom_call_target="tpu_custom_call" | custom-call | flops 12000000000 | bytes 15000000 | tf_op jit(solution)/shard_map/pallas_call | solution.py:36
  117.8 17.2 %shard_map.100 = (bf16[4,4,128,128]{3,2,1,0:T(8,128)(2,1)}, bf16[4,4,128,128]{3,2,1,0:T(8,128)(2,1)}, f32[128,2048]{1,0:T(8,128)}) custom-call(bf16[4,4,128,128]{3,2,1,0:T(8,128)(2,1)} %collective-permute-done.7.refs_2_.same_ref, bf16[4,4,128,128]{3,2,1,0:T(8,128)(2,1)} %collective-permute-done.8.refs_2_.other_ref, ...), custom_call_target="tpu_custom_call" | custom-call | flops 12800000000 | bytes 16000000 | tf_op jit(solution)/shard_map/pallas_call | solution.py:36
  135.3 17.6 %shard_map.101 = (bf16[4,4,128,128]{3,2,1,0:T(8,128)(2,1)}, bf16[4,4,128,128]{3,2,1,0:T(8,128)(2,1)}, f32[128,2048]{1,0:T(8,128)}) custom-call(bf16[4,4,128,128]{3,2,1,0:T(8,128)(2,1)} %copy-done.14, bf16[4,4,128,128]{3,2,1,0:T(8,128)(2,1)} %collective-permute-done.4.refs_0_.other_ref, bf16[2048,128]{1,0:T(8,128)(2,1)} %get-tuple-element.27.refs_3_.query_ref, ...), custom_call_target="tpu_custom_call" | custom-call | flops 12800000000 | bytes 16000000 | tf_op jit(solution)/shard_map/pallas_call | solution.py:36
  153.1 17.7 %shard_map.102 = (bf16[4,4,128,128]{3,2,1,0:T(8,128)(2,1)}, bf16[4,4,128,128]{3,2,1,0:T(8,128)(2,1)}, f32[128,2048]{1,0:T(8,128)}) custom-call(bf16[4,4,128,128]{3,2,1,0:T(8,128)(2,1)} %copy-done.13, bf16[4,4,128,128]{3,2,1,0:T(8,128)(2,1)} %copy-done.15, bf16[2048,128]{1,0:T(8,128)(2,1)} %get-tuple-element.27.refs_3_.query_ref, ...), custom_call_target="tpu_custom_call" | custom-call | flops 12800000000 | bytes 16000000 | tf_op jit(solution)/shard_map/pallas_call | solution.py:36
  171.0 17.4 %shard_map.103 = (bf16[4,4,128,128]{3,2,1,0:T(8,128)(2,1)}, bf16[4,4,128,128]{3,2,1,0:T(8,128)(2,1)}, bf16[1024,128]{1,0:T(8,128)(2,1)}) custom-call(bf16[4,4,128,128]{3,2,1,0:T(8,128)(2,1)} %bitcast.44, bf16[4,4,128,128]{3,2,1,0:T(8,128)(2,1)} %copy-done.12, bf16[2048,128]{1,0:T(8,128)(2,1)} %get-tuple-element.27.refs_3_.query_ref, ...), custom_call_target="tpu_custom_call" | custom-call | flops 12800000000 | bytes 16000000 | tf_op jit(solution)/shard_map/pallas_call | solution.py:36
  188.7 6.2 %all-to-all-start.2 = ((bf16[128,8,128]{2,1,0:T(8,128)(2,1)}), bf16[128,8,128]{2,1,0:T(8,128)(2,1)S(1)}, u32[]{:S(2)}, u32[]{:S(2)}) async-start(bf16[128,8,128]{2,1,0:T(8,128)(2,1)} %bitcast.10), calls=%async_computation.2 | async-start | bytes 524288 | tf_op jit(solution)/shard_map/all_to_all | solution.py:374
  195.0 2.9 %collective-permute-start.14 = (bf16[4,4,128,128]{3,2,1,0:T(8,128)(2,1)S(1)}, bf16[4,4,128,128]{3,2,1,0:T(8,128)(2,1)S(1)}, u32[]{:S(2)}, u32[]{:S(2)}) collective-permute-start(bf16[4,4,128,128]{3,2,1,0:T(8,128)(2,1)S(1)} %add_convert_fusion.3), channel_id=1, source_target_pairs={{0,64},{32,96},{64,0},{96,32},{1,65},{33,97},{65,1},{97,33},{2,66}... | collective-permute-start | bytes 1572872 | tf_op jit(solution)/shard_map/ppermute | solution.py:351
  200.1 5.6 %all-to-all-done.2 = bf16[128,8,128]{2,1,0:T(8,128)(2,1)S(1)} async-done(((bf16[128,8,128]{2,1,0:T(8,128)(2,1)}), bf16[128,8,128]{2,1,0:T(8,128)(2,1)S(1)}, u32[]{:S(2)}, u32[]{:S(2)}) %all-to-all-start.2) | async-done | bytes 262176 | tf_op jit(solution)/shard_map/all_to_all | solution.py:374
  206.4 2.4 shard_map.98
  212.0 3.7 %collective-permute-start.11 = (bf16[1,2,32,512]{3,2,1,0:T(8,128)(2,1)S(1)}, bf16[1,2,32,512]{3,2,1,0:T(8,128)(2,1)S(1)}, u32[]{:S(2)}, u32[]{:S(2)}) collective-permute-start(bf16[1,2,32,512]{3,2,1,0:T(8,128)(2,1)S(1)} %bitcast.60), channel_id=1, source_target_pairs={{0,7},{1,0},{2,1},{3,2},{4,3},{5,4},{6,5},{7,6},{8,15},{9,8},{10,9... | collective-permute-start | bytes 196616 | tf_op jit(solution)/shard_map/ppermute | solution.py:363
  217.6 2.9 %collective-permute-start.12 = (bf16[4,2,32,512]{3,2,1,0:T(8,128)(2,1)S(1)}, bf16[4,2,32,512]{3,2,1,0:T(8,128)(2,1)}, u32[]{:S(2)}, u32[]{:S(2)}) collective-permute-start(bf16[4,2,32,512]{3,2,1,0:T(8,128)(2,1)S(1)} %pad_maximum_fusion.2.own_ref), channel_id=1, source_target_pairs={{0,8},{8,16},{16,24},{24,32},{32,40},{40,48},{48,56},{56,64},{64,7... | collective-permute-start | bytes 786440 | tf_op jit(solution)/shard_map/ppermute | solution.py:369
  220.5 2.6 collective-permute-done.16
  226.5 11.4 %all-to-all-start.3 = ((bf16[128,24,128]{2,1,0:T(8,128)(2,1)}), bf16[128,24,128]{2,1,0:T(8,128)(2,1)S(1)}, u32[]{:S(2)}, u32[]{:S(2)}) async-start(bf16[128,24,128]{2,1,0:T(8,128)(2,1)} %pad_maximum_fusion), calls=%async_computation.3 | async-start | bytes 1572864 | tf_op jit(solution)/shard_map/all_to_all | solution.py:374
  237.9 10.2 %shard_map.99 = bf16[128,512]{1,0:T(8,128)(2,1)} custom-call(bf16[4,2,32,512]{3,2,1,0:T(8,128)(2,1)} %copy-done.9, bf16[4,2,32,512]{3,2,1,0:T(8,128)(2,1)} %collective-permute-done.12.near_ref, bf16[3,3,3,512,512]{4,3,2,1,0:T(8,128)(2,1)} %taps_ref.3), custom_call_target="tpu_custom_call" | custom-call | flops 8000000000 | bytes 10000000 | tf_op jit(solution)/shard_map/pallas_call | solution.py:36
  249.8 4.3 %all-to-all-done.3 = bf16[128,24,128]{2,1,0:T(8,128)(2,1)S(1)} async-done(((bf16[128,24,128]{2,1,0:T(8,128)(2,1)}), bf16[128,24,128]{2,1,0:T(8,128)(2,1)S(1)}, u32[]{:S(2)}, u32[]{:S(2)}) %all-to-all-start.3) | async-done | bytes 786464 | tf_op jit(solution)/shard_map/all_to_all | solution.py:374
  255.0 2.3 shard_map.104
  257.4 1.9 copy.23
  259.3 2.4 copy_bitcast_fusion
  (80 shorter events, 22.2 us)
Async XLA Ops:
  0.6 7.4 %copy-start.6 = (bf16[2,32,2,1024]{3,2,1,0:T(2,128)(2,1)S(1)}, bf16[2,32,2,1024]{3,2,1,0:T(2,128)(2,1)}, u32[]{:S(2)}) copy-start(bf16[2,32,2,1024]{3,2,1,0:T(2,128)(2,1)} %param.8) | copy-start | bytes 786436
  1.6 7.2 %collective-permute-start = (bf16[1,2,32,512]{3,2,1,0:T(8,128)(2,1)S(1)}, bf16[1,2,32,512]{3,2,1,0:T(8,128)(2,1)S(1)}, u32[]{:S(2)}, u32[]{:S(2)}) collective-permute-start(bf16[1,2,32,512]{3,2,1,0:T(8,128)(2,1)S(1)} %get-tuple-element.50), channel_id=1, source_target_pairs={{0,1},{1,2},{2,3},{3,4},{4,5},{5,6},{6,7},{7,0},{8,9},{9,10},{10,1... | collective-permute-start | bytes 196616 | tf_op jit(solution)/shard_map/ppermute | solution.py:363
  4.7 4.2 %collective-permute-start.1 = (bf16[1,2,32,512]{3,2,1,0:T(8,128)(2,1)S(1)}, bf16[1,2,32,512]{3,2,1,0:T(8,128)(2,1)S(1)}, u32[]{:S(2)}, u32[]{:S(2)}) collective-permute-start(bf16[1,2,32,512]{3,2,1,0:T(8,128)(2,1)S(1)} %get-tuple-element.51), channel_id=1, source_target_pairs={{0,7},{1,0},{2,1},{3,2},{4,3},{5,4},{6,5},{7,6},{8,15},{9,8},{10,9... | collective-permute-start | bytes 196616 | tf_op jit(solution)/shard_map/ppermute | solution.py:363
  8.9 15.1 %collective-permute-start.2 = (bf16[4,2,32,512]{3,2,1,0:T(8,128)(2,1)S(1)}, bf16[4,2,32,512]{3,2,1,0:T(8,128)(2,1)S(1)}, u32[]{:S(2)}, u32[]{:S(2)}) collective-permute-start(bf16[4,2,32,512]{3,2,1,0:T(8,128)(2,1)S(1)} %pad_maximum_fusion.1.own_ref), channel_id=1, source_target_pairs={{8,0},{16,8},{24,16},{32,24},{40,32},{48,40},{56,48},{64,56},{72,6... | collective-permute-start | bytes 786440 | tf_op jit(solution)/shard_map/ppermute | solution.py:369
  12.6 27.6 %all-to-all-start = ((bf16[128,24,128]{2,1,0:T(8,128)(2,1)}), bf16[128,24,128]{2,1,0:T(8,128)(2,1)S(1)}, u32[]{:S(2)}, u32[]{:S(2)}) async-start(bf16[128,24,128]{2,1,0:T(8,128)(2,1)} %bitcast.38), calls=%async_computation | async-start | bytes 1572864 | tf_op jit(solution)/shard_map/all_to_all | solution.py:374
  40.3 30.0 %copy-start.4 = (bf16[128,16,128]{2,1,0:T(8,128)(2,1)}, bf16[128,16,128]{2,1,0:T(8,128)(2,1)S(1)}, u32[]{:S(2)}) copy-start(bf16[128,16,128]{2,1,0:T(8,128)(2,1)S(1)} %slice.26) | copy-start | bytes 1572868
  40.3 14.2 %collective-permute-start.3 = (bf16[4,4,128,128]{3,2,1,0:T(8,128)(2,1)S(1)}, bf16[4,4,128,128]{3,2,1,0:T(8,128)(2,1)S(1)}, u32[]{:S(2)}, u32[]{:S(2)}) collective-permute-start(bf16[4,4,128,128]{3,2,1,0:T(8,128)(2,1)S(1)} %bitcast.39), channel_id=1, source_target_pairs={{0,32},{32,64},{64,96},{96,0},{1,33},{33,65},{65,97},{97,1},{2,34}... | collective-permute-start | bytes 1572872 | tf_op jit(solution)/shard_map/ppermute | solution.py:351
  40.7 29.1 %collective-permute-start.5 = (bf16[4,4,128,128]{3,2,1,0:T(8,128)(2,1)S(1)}, bf16[4,4,128,128]{3,2,1,0:T(8,128)(2,1)S(1)}, u32[]{:S(2)}, u32[]{:S(2)}) collective-permute-start(bf16[4,4,128,128]{3,2,1,0:T(8,128)(2,1)S(1)} %bitcast.40), channel_id=1, source_target_pairs={{0,96},{32,0},{64,32},{96,64},{1,97},{33,1},{65,33},{97,65},{2,98}... | collective-permute-start | bytes 1572872 | tf_op jit(solution)/shard_map/ppermute | solution.py:351
  43.0 26.8 %collective-permute-start.7 = (bf16[4,4,128,128]{3,2,1,0:T(8,128)(2,1)S(1)}, bf16[4,4,128,128]{3,2,1,0:T(8,128)(2,1)}, u32[]{:S(2)}, u32[]{:S(2)}) collective-permute-start(bf16[4,4,128,128]{3,2,1,0:T(8,128)(2,1)S(1)} %bitcast.41), channel_id=1, source_target_pairs={{0,64},{32,96},{64,0},{96,32},{1,65},{33,97},{65,1},{97,33},{2,66}... | collective-permute-start | bytes 1572872 | tf_op jit(solution)/shard_map/ppermute | solution.py:351
  43.0 27.3 %collective-permute-start.9 = (bf16[4,4,128,128]{3,2,1,0:T(8,128)(2,1)S(1)}, bf16[4,4,128,128]{3,2,1,0:T(8,128)(2,1)S(1)}, u32[]{:S(2)}, u32[]{:S(2)}) collective-permute-start(bf16[4,4,128,128]{3,2,1,0:T(8,128)(2,1)S(1)} %bitcast.42), channel_id=1, source_target_pairs={{0,1},{1,0},{2,3},{3,2},{4,5},{5,4},{6,7},{7,6},{8,9},{9,8},{10,11... | collective-permute-start | bytes 1572872 | tf_op jit(solution)/shard_map/ppermute | solution.py:355
  45.6 53.7 %all-to-all-start.1 = ((bf16[128,8,128]{2,1,0:T(8,128)(2,1)}), bf16[128,8,128]{2,1,0:T(8,128)(2,1)S(1)}, u32[]{:S(2)}, u32[]{:S(2)}) async-start(bf16[128,8,128]{2,1,0:T(8,128)(2,1)} %bitcast.9), calls=%async_computation.1 | async-start | bytes 524288 | tf_op jit(solution)/shard_map/all_to_all | solution.py:374
  54.5 28.6 %copy-start.14 = (bf16[4,4,128,128]{3,2,1,0:T(8,128)(2,1)}, bf16[4,4,128,128]{3,2,1,0:T(8,128)(2,1)S(1)}, u32[]{:S(2)}) copy-start(bf16[4,4,128,128]{3,2,1,0:T(8,128)(2,1)S(1)} %collective-permute-done.3.refs_0_.same_ref) | copy-start | bytes 1572868
  54.5 44.9 %collective-permute-start.4 = (bf16[4,4,128,128]{3,2,1,0:T(8,128)(2,1)S(1)}, bf16[4,4,128,128]{3,2,1,0:T(8,128)(2,1)}, u32[]{:S(2)}, u32[]{:S(2)}) collective-permute-start(bf16[4,4,128,128]{3,2,1,0:T(8,128)(2,1)S(1)} %collective-permute-done.3.refs_0_.same_ref), channel_id=1, source_target_pairs={{0,1},{1,0},{2,3},{3,2},{4,5},{5,4},{6,7},{7,6},{8,9},{9,8},{10,11... | collective-permute-start | bytes 1572872 | tf_op jit(solution)/shard_map/ppermute | solution.py:355
  69.8 13.3 %copy-start.13 = (bf16[4,4,128,128]{3,2,1,0:T(8,128)(2,1)}, bf16[4,4,128,128]{3,2,1,0:T(8,128)(2,1)S(1)}, u32[]{:S(2)}) copy-start(bf16[4,4,128,128]{3,2,1,0:T(8,128)(2,1)S(1)} %collective-permute-done.5.refs_1_.same_ref) | copy-start | bytes 1572868
  69.8 29.6 %collective-permute-start.6 = (bf16[4,4,128,128]{3,2,1,0:T(8,128)(2,1)S(1)}, bf16[4,4,128,128]{3,2,1,0:T(8,128)(2,1)S(1)}, u32[]{:S(2)}, u32[]{:S(2)}) collective-permute-start(bf16[4,4,128,128]{3,2,1,0:T(8,128)(2,1)S(1)} %collective-permute-done.5.refs_1_.same_ref), channel_id=1, source_target_pairs={{0,1},{1,0},{2,3},{3,2},{4,5},{5,4},{6,7},{7,6},{8,9},{9,8},{10,11... | collective-permute-start | bytes 1572872 | tf_op jit(solution)/shard_map/ppermute | solution.py:355
  69.9 29.5 %collective-permute-start.8 = (bf16[4,4,128,128]{3,2,1,0:T(8,128)(2,1)}, bf16[4,4,128,128]{3,2,1,0:T(8,128)(2,1)}, u32[]{:S(2)}, u32[]{:S(2)}) collective-permute-start(bf16[4,4,128,128]{3,2,1,0:T(8,128)(2,1)} %collective-permute-done.7.refs_2_.same_ref), channel_id=1, source_target_pairs={{0,1},{1,0},{2,3},{3,2},{4,5},{5,4},{6,7},{7,6},{8,9},{9,8},{10,11... | collective-permute-start | bytes 1572872 | tf_op jit(solution)/shard_map/ppermute | solution.py:355
  135.0 59.8 %collective-permute-start.13 = (bf16[4,4,128,128]{3,2,1,0:T(8,128)(2,1)}, bf16[4,4,128,128]{3,2,1,0:T(8,128)(2,1)S(1)}, u32[]{:S(2)}, u32[]{:S(2)}) collective-permute-start(bf16[4,4,128,128]{3,2,1,0:T(8,128)(2,1)} %get-tuple-element.38), channel_id=1, source_target_pairs={{0,1},{1,0},{2,3},{3,2},{4,5},{5,4},{6,7},{7,6},{8,9},{9,8},{10,11... | collective-permute-start | bytes 1572872 | tf_op jit(solution)/shard_map/ppermute | solution.py:355
  152.9 45.1 %collective-permute-start.15 = (bf16[4,4,128,128]{3,2,1,0:T(8,128)(2,1)}, bf16[4,4,128,128]{3,2,1,0:T(8,128)(2,1)S(1)}, u32[]{:S(2)}, u32[]{:S(2)}) collective-permute-start(bf16[4,4,128,128]{3,2,1,0:T(8,128)(2,1)} %get-tuple-element.40), channel_id=1, source_target_pairs={{0,1},{1,0},{2,3},{3,2},{4,5},{5,4},{6,7},{7,6},{8,9},{9,8},{10,11... | collective-permute-start | bytes 1572872 | tf_op jit(solution)/shard_map/ppermute | solution.py:355
  170.8 28.3 %collective-permute-start.17 = (bf16[4,4,128,128]{3,2,1,0:T(8,128)(2,1)}, bf16[4,4,128,128]{3,2,1,0:T(8,128)(2,1)S(1)}, u32[]{:S(2)}, u32[]{:S(2)}) collective-permute-start(bf16[4,4,128,128]{3,2,1,0:T(8,128)(2,1)} %get-tuple-element.42), channel_id=1, source_target_pairs={{0,1},{1,0},{2,3},{3,2},{4,5},{5,4},{6,7},{7,6},{8,9},{9,8},{10,11... | collective-permute-start | bytes 1572872 | tf_op jit(solution)/shard_map/ppermute | solution.py:355
  171.0 23.8 %copy-start.3 = (bf16[4,4,128,128]{3,2,1,0:T(8,128)(2,1)S(1)}, bf16[4,4,128,128]{3,2,1,0:T(8,128)(2,1)}, u32[]{:S(2)}) copy-start(bf16[4,4,128,128]{3,2,1,0:T(8,128)(2,1)} %get-tuple-element.37) | copy-start | bytes 1572868
  188.4 9.5 %copy-start.2 = (bf16[4,4,128,128]{3,2,1,0:T(8,128)(2,1)S(1)}, bf16[4,4,128,128]{3,2,1,0:T(8,128)(2,1)}, u32[]{:S(2)}) copy-start(bf16[4,4,128,128]{3,2,1,0:T(8,128)(2,1)} %get-tuple-element.39) | copy-start | bytes 1572868
  188.4 32.1 %collective-permute-start.19 = (bf16[4,4,128,128]{3,2,1,0:T(8,128)(2,1)}, bf16[4,4,128,128]{3,2,1,0:T(8,128)(2,1)}, u32[]{:S(2)}, u32[]{:S(2)}) collective-permute-start(bf16[4,4,128,128]{3,2,1,0:T(8,128)(2,1)} %get-tuple-element.44), channel_id=1, source_target_pairs={{0,1},{1,0},{2,3},{3,2},{4,5},{5,4},{6,7},{7,6},{8,9},{9,8},{10,11... | collective-permute-start | bytes 1572872 | tf_op jit(solution)/shard_map/ppermute | solution.py:355
  188.7 17.0 %all-to-all-start.2 = ((bf16[128,8,128]{2,1,0:T(8,128)(2,1)}), bf16[128,8,128]{2,1,0:T(8,128)(2,1)S(1)}, u32[]{:S(2)}, u32[]{:S(2)}) async-start(bf16[128,8,128]{2,1,0:T(8,128)(2,1)} %bitcast.10), calls=%async_computation.2 | async-start | bytes 524288 | tf_op jit(solution)/shard_map/all_to_all | solution.py:374
  195.0 25.5 %collective-permute-start.14 = (bf16[4,4,128,128]{3,2,1,0:T(8,128)(2,1)S(1)}, bf16[4,4,128,128]{3,2,1,0:T(8,128)(2,1)S(1)}, u32[]{:S(2)}, u32[]{:S(2)}) collective-permute-start(bf16[4,4,128,128]{3,2,1,0:T(8,128)(2,1)S(1)} %add_convert_fusion.3), channel_id=1, source_target_pairs={{0,64},{32,96},{64,0},{96,32},{1,65},{33,97},{65,1},{97,33},{2,66}... | collective-permute-start | bytes 1572872 | tf_op jit(solution)/shard_map/ppermute | solution.py:351
  198.1 25.0 %collective-permute-start.16 = (bf16[4,4,128,128]{3,2,1,0:T(8,128)(2,1)S(1)}, bf16[4,4,128,128]{3,2,1,0:T(8,128)(2,1)S(1)}, u32[]{:S(2)}, u32[]{:S(2)}) collective-permute-start(bf16[4,4,128,128]{3,2,1,0:T(8,128)(2,1)S(1)} %add_convert_fusion.2), channel_id=1, source_target_pairs={{0,96},{32,0},{64,32},{96,64},{1,97},{33,1},{65,33},{97,65},{2,98}... | collective-permute-start | bytes 1572872 | tf_op jit(solution)/shard_map/ppermute | solution.py:351
  199.2 24.8 %collective-permute-start.18 = (bf16[4,4,128,128]{3,2,1,0:T(8,128)(2,1)S(1)}, bf16[4,4,128,128]{3,2,1,0:T(8,128)(2,1)S(1)}, u32[]{:S(2)}, u32[]{:S(2)}) collective-permute-start(bf16[4,4,128,128]{3,2,1,0:T(8,128)(2,1)S(1)} %add_convert_fusion.1), channel_id=1, source_target_pairs={{0,32},{32,64},{64,96},{96,0},{1,33},{33,65},{65,97},{97,1},{2,34}... | collective-permute-start | bytes 1572872 | tf_op jit(solution)/shard_map/ppermute | solution.py:351
  206.4 17.6 %copy-start.5 = (bf16[4,4,128,128]{3,2,1,0:T(8,128)(2,1)S(1)}, bf16[4,4,128,128]{3,2,1,0:T(8,128)(2,1)}, u32[]{:S(2)}) copy-start(bf16[4,4,128,128]{3,2,1,0:T(8,128)(2,1)} %get-tuple-element.43) | copy-start | bytes 1572868
  209.7 2.3 collective-permute-start.10
  212.0 4.6 %collective-permute-start.11 = (bf16[1,2,32,512]{3,2,1,0:T(8,128)(2,1)S(1)}, bf16[1,2,32,512]{3,2,1,0:T(8,128)(2,1)S(1)}, u32[]{:S(2)}, u32[]{:S(2)}) collective-permute-start(bf16[1,2,32,512]{3,2,1,0:T(8,128)(2,1)S(1)} %bitcast.60), channel_id=1, source_target_pairs={{0,7},{1,0},{2,1},{3,2},{4,3},{5,4},{6,5},{7,6},{8,15},{9,8},{10,9... | collective-permute-start | bytes 196616 | tf_op jit(solution)/shard_map/ppermute | solution.py:363
  217.5 7.9 %copy-start.9 = (bf16[4,2,32,512]{3,2,1,0:T(8,128)(2,1)}, bf16[4,2,32,512]{3,2,1,0:T(8,128)(2,1)S(1)}, u32[]{:S(2)}) copy-start(bf16[4,2,32,512]{3,2,1,0:T(8,128)(2,1)S(1)} %pad_maximum_fusion.2.own_ref) | copy-start | bytes 786436
  217.6 20.3 %collective-permute-start.12 = (bf16[4,2,32,512]{3,2,1,0:T(8,128)(2,1)S(1)}, bf16[4,2,32,512]{3,2,1,0:T(8,128)(2,1)}, u32[]{:S(2)}, u32[]{:S(2)}) collective-permute-start(bf16[4,2,32,512]{3,2,1,0:T(8,128)(2,1)S(1)} %pad_maximum_fusion.2.own_ref), channel_id=1, source_target_pairs={{0,8},{8,16},{16,24},{24,32},{32,40},{40,48},{48,56},{56,64},{64,7... | collective-permute-start | bytes 786440 | tf_op jit(solution)/shard_map/ppermute | solution.py:369
  226.5 27.7 %all-to-all-start.3 = ((bf16[128,24,128]{2,1,0:T(8,128)(2,1)}), bf16[128,24,128]{2,1,0:T(8,128)(2,1)S(1)}, u32[]{:S(2)}, u32[]{:S(2)}) async-start(bf16[128,24,128]{2,1,0:T(8,128)(2,1)} %pad_maximum_fusion), calls=%async_computation.3 | async-start | bytes 1572864 | tf_op jit(solution)/shard_map/all_to_all | solution.py:374
  (9 other events, 14.2 us)
where the time goes:
time: 263 us; the launch traced here: 262 us
  Pallas kernels  145 us (55%)
  starting transfers between devices  73.1 us (28%)
  waiting for transfers between devices  21.6 us (8%)
  local copies, waits for them, and re-layouts  16.8 us (6%)
  other arithmetic  3.87 us (1%)
    pallas_call x12, Pallas kernels, kernel_call(): pl.pallas_call(body, out_shape=outs, grid=grid, in_specs=in_specs, out_sp...  145 us
    all_to_all x4, starting transfers between devices, exchange_all(): return lax.all_to_all(split, AXES, split_axis=0, concat_axis=0, tiled=True)  34.9 us
    ppermute x8, starting transfers between devices, swap_core(): return lax.ppermute(value, 'c', [(0, 1), (1, 0)])  18.7 us
    all_to_all x4, waiting for transfers between devices, exchange_all(): return lax.all_to_all(split, AXES, split_axis=0, concat_axis=0, tiled=True)  13 us
    ppermute x4, starting transfers between devices, turn(): return lax.ppermute(value, ('z', 'c'), pairs)  7.7 us
    ppermute x6, starting transfers between devices, shift_y(): return lax.ppermute(value, 'y', [(i, (i + steps) % 4) for i in range(4)])  7.56 us
    ppermute x6, waiting for transfers between devices, shift_y(): return lax.ppermute(value, 'y', [(i, (i + steps) % 4) for i in range(4)])  6.4 us
  transfers between devices with their start and end apart: 24, of which 8 were waited for; matrix products, arithmetic and copies ran while one was open for 4% of the time, Pallas kernels for 41%

commit v1 on v0

--- a/solution.py
+++ b/solution.py
@@ -60,9 +60,7 @@
 def write_columns(tile_of, out_ref, stage_ref, place):
     lane = lax.broadcasted_iota(jnp.int32, (1, 128), 1)
     for tile in range(8):
-        value = tile_of(tile)
-        first = value[: 2 * ROWS]
-        second = value[2 * ROWS :]
+        first, second = tile_of(tile)
         even = jnp.where(lane < HEAD, first, pltpu.roll(second, HEAD, 1))
         odd = jnp.where(lane < HEAD, pltpu.roll(first, HEAD, 1), second)
         write_rows(even, 2 * tile, place, out_ref, stage_ref)
@@ -72,23 +70,11 @@
 def write_pairs(low, high, out_ref, stage_ref, place):
     lane = lax.broadcasted_iota(jnp.int32, (1, 128), 1)
     for tile in range(8):
-        a = low(tile)
-        b = high(tile)
-        even = jnp.where(lane < HEAD, a, pltpu.roll(b, HEAD, 1))
-        odd = jnp.where(lane < HEAD, pltpu.roll(a, HEAD, 1), b)
-        for half, value in ((0, even), (1, odd)):
-            for col in range(2):
-                part = value[col * 2 * ROWS : (col + 1) * 2 * ROWS]
-                write_rows(part, 2 * tile + half, place + col, out_ref, stage_ref)
-
-
-def read_rows(value, slot, col, tile, target, stage_ref):
-    stage_ref[slot] = value
-    for frame in range(2):
-        row = (col * 2 + frame) * ROWS
-        target[row : row + ROWS, tile * 128 : (tile + 1) * 128] = stage_ref[
-            slot, pl.ds(frame, ROWS, stride=2), :
-        ].astype(BF)
+        for col, (a, b) in enumerate(zip(low(tile), high(tile))):
+            even = jnp.where(lane < HEAD, a, pltpu.roll(b, HEAD, 1))
+            odd = jnp.where(lane < HEAD, pltpu.roll(a, HEAD, 1), b)
+            write_rows(even, 2 * tile, place + col, out_ref, stage_ref)
+            write_rows(odd, 2 * tile + 1, place + col, out_ref, stage_ref)
 
 
 def heads_of(in_ref, tile, place):
@@ -100,23 +86,24 @@
     return low, high
 
 
-def read_columns(in_ref, target, stage_ref, place):
-    for tile in range(8):
-        low, high = heads_of(in_ref, tile, place)
-        read_rows(low, 2 * tile, 0, tile, target, stage_ref)
-        read_rows(high, 2 * tile + 1, 1, tile, target, stage_ref)
-
-
-def read_pairs(in_ref, low_ref, high_ref, stage_ref, place):
-    for tile in range(8):
-        for col in range(2):
-            low, high = heads_of(in_ref, tile, place + col)
-            read_rows(low, 2 * tile, col, tile, low_ref, stage_ref)
-            read_rows(high, 2 * tile + 1, col, tile, high_ref, stage_ref)
+def frame_rows(values, tile, stage_ref):
+    for col in range(2):
+        stage_ref[2 * tile + col] = values[col]
+    for frame in range(2):
+        yield frame, [stage_ref[2 * tile + col, pl.ds(frame, ROWS, stride=2), :] for col in range(2)]
+
+
+def store_tokens(values, tile, target, stage_ref):
+    for frame, cols in frame_rows(values, tile, stage_ref):
+        target[frame * ROWS : (frame + 1) * ROWS, :, tile * 128 : (tile + 1) * 128] = jnp.stack(
+            cols, axis=1
+        ).astype(BF)
 
 
 def tiles_of(ref):
-    return lambda tile: ref[:, tile * 128 : (tile + 1) * 128].astype(F32)
+    return lambda tile: [
+        ref[:, col, tile * 128 : (tile + 1) * 128].astype(F32) for col in range(2)
+    ]
 
 
 def pack_body(q_ref, k_ref, v_ref, out_ref, stage_ref):
@@ -174,19 +161,28 @@
         grad = acc_ref[...].astype(BF)
 
         def tile_of(tile):
-            return dot(grad, proj_ref[tile * 128 : (tile + 1) * 128, :], NT)
+            value = dot(grad, proj_ref[tile * 128 : (tile + 1) * 128, :], NT)
+            return value[: 2 * ROWS], value[2 * ROWS :]
 
         write_columns(tile_of, out_ref, stage_ref, 0)
 
 
 def project_body(in_ref, proj_ref, out_ref, att_ref, stage_ref):
-    read_columns(in_ref, att_ref, stage_ref, 0)
+    for tile in range(8):
+        for frame, cols in frame_rows(heads_of(in_ref, tile, 0), tile, stage_ref):
+            for col in range(2):
+                row = (col * 2 + frame) * ROWS
+                att_ref[row : row + ROWS, tile * 128 : (tile + 1) * 128] = cols[col].astype(BF)
     out_ref[...] = dot(att_ref[...], proj_ref[...]).astype(BF)
 
 
 def unpack_body(in_ref, gq_ref, gk_ref, gv_ref, stage_ref):
-    read_columns(in_ref, gq_ref, stage_ref, 0)
-    read_pairs(in_ref, gk_ref, gv_ref, stage_ref, 1)
+    for tile in range(8):
+        store_tokens(heads_of(in_ref, tile, 0), tile, gq_ref, stage_ref.at[0])
+        first = heads_of(in_ref, tile, 1)
+        second = heads_of(in_ref, tile, 2)
+        store_tokens((first[0], second[0]), tile, gk_ref, stage_ref.at[1])
+        store_tokens((first[1], second[1]), tile, gv_ref, stage_ref.at[2])
 
 
 def join_columns(value, out_ref, base, roll_low):
@@ -379,7 +375,7 @@
 
 
 def flat(array):
-    return columns_first(array).reshape(4 * ROWS, -1)
+    return array.reshape(2 * ROWS, 2, -1)
 
 
 def tokens_back(array):
@@ -442,12 +438,12 @@
     query, seed = attend(
         [kv_same[0], kv_other[0]], (source,), [struct((SPAN, 128)), state], 10.0, True
     )
-    (seed,) = attend([kv_same[i] for i in (1, 3, 2)], (query, seed), [state], 15.0)
+    rest = [kv_same[i] for i in (1, 3, 2)] + [kv_other[i] for i in (1, 3, 2)]
     att, stats, grad = attend(
-        [kv_other[i] for i in (1, 3, 2)],
+        rest,
         (query, seed, grad),
         [struct((SPAN // 2, 128)), struct((8, SPAN), F32), struct((SPAN, 128))],
-        15.0,
+        25.0,
         last=True,
     )
     att = exchange_all(att).reshape(4, 16, 2, 1, 8, 128)
@@ -498,8 +494,14 @@
         [seed.reshape(128, 8, 128), total.astype(BF).reshape(128, 16, 128)], axis=1
     )
     grads = exchange_all(grads).reshape(4, 16, 2, 3, 8, 128)
-    grads = kernel_call(unpack_body, [struct((4 * ROWS, 1024))] * 3, [stage], (grads,), us=4.0)
-    return (tokens_back(conv), *(tokens_back(g) for g in grads))
+    grads = kernel_call(
+        unpack_body,
+        [struct((2 * ROWS, 2, 1024))] * 3,
+        [pltpu.VMEM((3, 16, 2 * ROWS, 128), F32)],
+        (grads,),
+        us=4.0,
+    )
+    return (tokens_back(conv), *(g.reshape(queries.shape) for g in grads))
 
 
 def solution(mesh):

time: 263 us -> 252 us (0.958)
  local copies, waits for them, and re-layouts: 16.8 us -> 8.29 us
  Pallas kernels: 145 us -> 140 us
  waiting for transfers between devices: 21.6 us -> 25.3 us
    transpose x4 -> x0, local copies, waits for them, and re-layouts: 6.52 us -> none  [the longest x3 4.17 us: columns_first(): return array.transpose(2, 0, 1, 3)]
    pallas_call x12 -> x11, Pallas kernels: 145 us -> 140 us  [kernel_call(): pl.pallas_call(body, out_shape=outs, grid=grid, in_specs=in_specs, out_sp...]
    ppermute x4, waiting for transfers between devices: 2.24 us -> 5.92 us  [turn(): return lax.ppermute(value, ('z', 'c'), pairs)]
  transfers between devices with their start and end apart: 24 -> 24, of which waited for: 8 -> 10; matrix products, arithmetic and copies ran while one was open for 4% -> 3% of each run, Pallas kernels for 41% -> 37%
where the time goes in v1:
time: 252 us; the launch traced here: 251 us
  Pallas kernels  140 us (56%)
  starting transfers between devices  72.2 us (29%)
  waiting for transfers between devices  25.3 us (10%)
  local copies, waits for them, and re-layouts  8.29 us (3%)
  other arithmetic  3.88 us (2%)
    pallas_call x11, Pallas kernels, kernel_call(): pl.pallas_call(body, out_shape=outs, grid=grid, in_specs=in_specs, out_sp...  140 us
    all_to_all x4, starting transfers between devices, exchange_all(): return lax.all_to_all(split, AXES, split_axis=0, concat_axis=0, tiled=True)  34 us
    ppermute x8, starting transfers between devices, swap_core(): return lax.ppermute(value, 'c', [(0, 1), (1, 0)])  18.7 us
    all_to_all x4, waiting for transfers between devices, exchange_all(): return lax.all_to_all(split, AXES, split_axis=0, concat_axis=0, tiled=True)  13 us
    ppermute x4, starting transfers between devices, turn(): return lax.ppermute(value, ('z', 'c'), pairs)  7.7 us
    ppermute x6, starting transfers between devices, shift_y(): return lax.ppermute(value, 'y', [(i, (i + steps) % 4) for i in range(4)])  7.56 us
    ppermute x6, waiting for transfers between devices, shift_y(): return lax.ppermute(value, 'y', [(i, (i + steps) % 4) for i in range(4)])  6.4 us
    ppermute x4, waiting for transfers between devices, turn(): return lax.ppermute(value, ('z', 'c'), pairs)  5.92 us
  transfers between devices with their start and end apart: 24, of which 10 were waited for; matrix products, arithmetic and copies ran while one was open for 3% of the time, Pallas kernels for 37%

profile of v1, /device:TPU:1, one launch (start us, length us, event | category | flops | bytes accessed | tf_op | source)
XLA Modules:
  0.0 250.8 jit_solution(11097407620486938947)
XLA Ops:
  1.6 3.0 %collective-permute-start = (bf16[1,2,32,512]{3,2,1,0:T(8,128)(2,1)S(1)}, bf16[1,2,32,512]{3,2,1,0:T(8,128)(2,1)S(1)}, u32[]{:S(2)}, u32[]{:S(2)}) collective-permute-start(bf16[1,2,32,512]{3,2,1,0:T(8,128)(2,1)S(1)} %get-tuple-element.50), channel_id=1, source_target_pairs={{0,1},{1,2},{2,3},{3,4},{4,5},{5,6},{6,7},{7,0},{8,9},{9,10},{10,1... | collective-permute-start | bytes 196616 | tf_op jit(solution)/shard_map/ppermute | solution.py:359
  4.6 1.3 collective-permute-done
  5.9 2.4 collective-permute-done.1
  9.6 3.8 %shard_map.93 = bf16[4,16,2,3,8,128]{5,4,3,2,1,0:T(8,128)(2,1)} custom-call(bf16[64,2,1024]{2,1,0:T(2,128)(2,1)} %bitcast.42, bf16[64,2,1024]{2,1,0:T(2,128)(2,1)} %bitcast.43, bf16[64,2,1024]{2,1,0:T(2,128)(2,1)} %bitcast.44), custom_call_target="tpu_custom_call" | custom-call | flops 3200000000 | bytes 4000000 | tf_op jit(solution)/shard_map/pallas_call | solution.py:36
  13.5 10.6 %all-to-all-start = ((bf16[128,24,128]{2,1,0:T(8,128)(2,1)}), bf16[128,24,128]{2,1,0:T(8,128)(2,1)S(1)}, u32[]{:S(2)}, u32[]{:S(2)}) async-start(bf16[128,24,128]{2,1,0:T(8,128)(2,1)} %bitcast.28), calls=%async_computation | async-start | bytes 1572864 | tf_op jit(solution)/shard_map/all_to_all | solution.py:370
  24.7 12.4 %shard_map.94 = bf16[4,16,2,1,8,128]{5,4,3,2,1,0:T(8,128)(2,1)} custom-call(bf16[4,2,32,512]{3,2,1,0:T(8,128)(2,1)} %copy-done.9, bf16[4,2,32,512]{3,2,1,0:T(8,128)(2,1)} %copy-done.15, bf16[3,3,3,512,512]{4,3,2,1,0:T(8,128)(2,1)} %taps_ref.3, bf16[1024,512]{1,0:T(8,128)(2,1)} %proj_ref.3), custom_call_target="tpu_custom_call" | custom-call | flops 9600000000 | bytes 12000000 | tf_op jit(solution)/shard_map/pallas_call | solution.py:36
  37.2 3.1 %all-to-all-done = bf16[128,24,128]{2,1,0:T(8,128)(2,1)S(1)} async-done(((bf16[128,24,128]{2,1,0:T(8,128)(2,1)}), bf16[128,24,128]{2,1,0:T(8,128)(2,1)S(1)}, u32[]{:S(2)}, u32[]{:S(2)}) %all-to-all-start) | async-done | bytes 786464 | tf_op jit(solution)/shard_map/all_to_all | solution.py:370
  40.7 2.3 collective-permute-start.4
  43.1 1.9 collective-permute-start.9
  45.6 5.9 %all-to-all-start.1 = ((bf16[128,8,128]{2,1,0:T(8,128)(2,1)}), bf16[128,8,128]{2,1,0:T(8,128)(2,1)S(1)}, u32[]{:S(2)}, u32[]{:S(2)}) async-start(bf16[128,8,128]{2,1,0:T(8,128)(2,1)} %bitcast.6), calls=%async_computation.1 | async-start | bytes 524288 | tf_op jit(solution)/shard_map/all_to_all | solution.py:370
  51.6 2.9 %collective-permute-done.3.refs_0_.same_ref = bf16[4,4,128,128]{3,2,1,0:T(8,128)(2,1)S(1)} collective-permute-done((bf16[4,4,128,128]{3,2,1,0:T(8,128)(2,1)S(1)}, bf16[4,4,128,128]{3,2,1,0:T(8,128)(2,1)S(1)}, u32[]{:S(2)}, u32[]{:S(2)}) %collective-permute-start.3) | collective-permute-done | bytes 524320 | tf_op jit(solution)/shard_map/ppermute | solution.py:347
  54.5 15.3 %collective-permute-start.6 = (bf16[4,4,128,128]{3,2,1,0:T(8,128)(2,1)S(1)}, bf16[4,4,128,128]{3,2,1,0:T(8,128)(2,1)}, u32[]{:S(2)}, u32[]{:S(2)}) collective-permute-start(bf16[4,4,128,128]{3,2,1,0:T(8,128)(2,1)S(1)} %collective-permute-done.3.refs_0_.same_ref), channel_id=1, source_target_pairs={{0,1},{1,0},{2,3},{3,2},{4,5},{5,4},{6,7},{7,6},{8,9},{9,8},{10,11... | collective-permute-start | bytes 1572872 | tf_op jit(solution)/shard_map/ppermute | solution.py:351
  71.1 12.0 %shard_map.95 = (bf16[2048,128]{1,0:T(8,128)(2,1)}, f32[2048,128]{1,0:T(8,128)}) custom-call(bf16[4,4,128,128]{3,2,1,0:T(8,128)(2,1)} %bitcast.33, bf16[4,4,128,128]{3,2,1,0:T(8,128)(2,1)} %copy-done.11, bf16[128,8,128]{2,1,0:T(8,128)(2,1)} %slice.27.refs_2_), custom_call_target="tpu_custom_call" | custom-call | flops 8000000000 | bytes 10000000 | tf_op jit(solution)/shard_map/pallas_call | solution.py:36
  84.1 25.7 %shard_map.96 = (bf16[1024,128]{1,0:T(8,128)(2,1)}, f32[8,2048]{1,0:T(8,128)}, bf16[2048,128]{1,0:T(8,128)(2,1)}) custom-call(bf16[4,4,128,128]{3,2,1,0:T(8,128)(2,1)} %copy-done.13, bf16[4,4,128,128]{3,2,1,0:T(8,128)(2,1)} %copy-done.12, bf16[4,4,128,128]{3,2,1,0:T(8,128)(2,1)} %collective-permute-done.5.refs_2_.same_ref, ...), custom_call_target="tpu_custom_call" | custom-call | flops 20000000000 | bytes 25000000 | tf_op jit(solution)/shard_map/pallas_call | solution.py:36
  109.9 17.2 %shard_map.99 = (bf16[4,4,128,128]{3,2,1,0:T(8,128)(2,1)}, bf16[4,4,128,128]{3,2,1,0:T(8,128)(2,1)}, f32[128,2048]{1,0:T(8,128)}) custom-call(bf16[4,4,128,128]{3,2,1,0:T(8,128)(2,1)} %collective-permute-done.5.refs_2_.same_ref, bf16[4,4,128,128]{3,2,1,0:T(8,128)(2,1)} %collective-permute-done.8.refs_5_.other_ref, ...), custom_call_target="tpu_custom_call" | custom-call | flops 12800000000 | bytes 16000000 | tf_op jit(solution)/shard_map/pallas_call | solution.py:36
  127.4 17.6 %shard_map.100 = (bf16[4,4,128,128]{3,2,1,0:T(8,128)(2,1)}, bf16[4,4,128,128]{3,2,1,0:T(8,128)(2,1)}, f32[128,2048]{1,0:T(8,128)}) custom-call(bf16[4,4,128,128]{3,2,1,0:T(8,128)(2,1)} %copy-done.13, bf16[4,4,128,128]{3,2,1,0:T(8,128)(2,1)} %collective-permute-done.6.refs_3_.other_ref, bf16[2048,128]{1,0:T(8,128)(2,1)} %get-tuple-element.27.refs_6_.query_ref, ...), custom_call_target="tpu_custom_call" | custom-call | flops 12800000000 | bytes 16000000 | tf_op jit(solution)/shard_map/pallas_call | solution.py:36
  145.2 17.6 %shard_map.101 = (bf16[4,4,128,128]{3,2,1,0:T(8,128)(2,1)}, bf16[4,4,128,128]{3,2,1,0:T(8,128)(2,1)}, f32[128,2048]{1,0:T(8,128)}) custom-call(bf16[4,4,128,128]{3,2,1,0:T(8,128)(2,1)} %copy-done.12, bf16[4,4,128,128]{3,2,1,0:T(8,128)(2,1)} %copy-done.14, bf16[2048,128]{1,0:T(8,128)(2,1)} %get-tuple-element.27.refs_6_.query_ref, ...), custom_call_target="tpu_custom_call" | custom-call | flops 12800000000 | bytes 16000000 | tf_op jit(solution)/shard_map/pallas_call | solution.py:36
  163.1 17.4 %shard_map.102 = (bf16[4,4,128,128]{3,2,1,0:T(8,128)(2,1)}, bf16[4,4,128,128]{3,2,1,0:T(8,128)(2,1)}, bf16[1024,128]{1,0:T(8,128)(2,1)}) custom-call(bf16[4,4,128,128]{3,2,1,0:T(8,128)(2,1)} %bitcast.34, bf16[4,4,128,128]{3,2,1,0:T(8,128)(2,1)} %copy-done.11, bf16[2048,128]{1,0:T(8,128)(2,1)} %get-tuple-element.27.refs_6_.query_ref, ...), custom_call_target="tpu_custom_call" | custom-call | flops 12800000000 | bytes 16000000 | tf_op jit(solution)/shard_map/pallas_call | solution.py:36
  180.8 6.1 %all-to-all-start.2 = ((bf16[128,8,128]{2,1,0:T(8,128)(2,1)}), bf16[128,8,128]{2,1,0:T(8,128)(2,1)S(1)}, u32[]{:S(2)}, u32[]{:S(2)}) async-start(bf16[128,8,128]{2,1,0:T(8,128)(2,1)} %bitcast.7), calls=%async_computation.2 | async-start | bytes 524288 | tf_op jit(solution)/shard_map/all_to_all | solution.py:370
  187.1 2.9 %collective-permute-start.14 = (bf16[4,4,128,128]{3,2,1,0:T(8,128)(2,1)S(1)}, bf16[4,4,128,128]{3,2,1,0:T(8,128)(2,1)S(1)}, u32[]{:S(2)}, u32[]{:S(2)}) collective-permute-start(bf16[4,4,128,128]{3,2,1,0:T(8,128)(2,1)S(1)} %add_convert_fusion.3), channel_id=1, source_target_pairs={{0,64},{32,96},{64,0},{96,32},{1,65},{33,97},{65,1},{97,33},{2,66}... | collective-permute-start | bytes 1572872 | tf_op jit(solution)/shard_map/ppermute | solution.py:347
  192.2 5.6 %all-to-all-done.2 = bf16[128,8,128]{2,1,0:T(8,128)(2,1)S(1)} async-done(((bf16[128,8,128]{2,1,0:T(8,128)(2,1)}), bf16[128,8,128]{2,1,0:T(8,128)(2,1)S(1)}, u32[]{:S(2)}, u32[]{:S(2)}) %all-to-all-start.2) | async-done | bytes 262176 | tf_op jit(solution)/shard_map/all_to_all | solution.py:370
  198.5 2.4 shard_map.97
  202.7 1.3 collective-permute-done.10
  204.1 3.7 %collective-permute-start.11 = (bf16[1,2,32,512]{3,2,1,0:T(8,128)(2,1)S(1)}, bf16[1,2,32,512]{3,2,1,0:T(8,128)(2,1)S(1)}, u32[]{:S(2)}, u32[]{:S(2)}) collective-permute-start(bf16[1,2,32,512]{3,2,1,0:T(8,128)(2,1)S(1)} %bitcast.40), channel_id=1, source_target_pairs={{0,7},{1,0},{2,1},{3,2},{4,3},{5,4},{6,5},{7,6},{8,15},{9,8},{10,9... | collective-permute-start | bytes 196616 | tf_op jit(solution)/shard_map/ppermute | solution.py:359
  209.6 2.9 %collective-permute-start.12 = (bf16[4,2,32,512]{3,2,1,0:T(8,128)(2,1)S(1)}, bf16[4,2,32,512]{3,2,1,0:T(8,128)(2,1)}, u32[]{:S(2)}, u32[]{:S(2)}) collective-permute-start(bf16[4,2,32,512]{3,2,1,0:T(8,128)(2,1)S(1)} %pad_maximum_fusion.2.own_ref), channel_id=1, source_target_pairs={{0,8},{8,16},{16,24},{24,32},{32,40},{40,48},{48,56},{56,64},{64,7... | collective-permute-start | bytes 786440 | tf_op jit(solution)/shard_map/ppermute | solution.py:365
  212.6 2.6 %collective-permute-done.16 = bf16[4,4,128,128]{3,2,1,0:T(8,128)(2,1)S(1)} collective-permute-done((bf16[4,4,128,128]{3,2,1,0:T(8,128)(2,1)S(1)}, bf16[4,4,128,128]{3,2,1,0:T(8,128)(2,1)S(1)}, u32[]{:S(2)}, u32[]{:S(2)}) %collective-permute-start.16) | collective-permute-done | bytes 524320 | tf_op jit(solution)/shard_map/ppermute | solution.py:347
  216.1 1.5 add_convert_fusion
  218.6 11.4 %all-to-all-start.3 = ((bf16[128,24,128]{2,1,0:T(8,128)(2,1)}), bf16[128,24,128]{2,1,0:T(8,128)(2,1)S(1)}, u32[]{:S(2)}, u32[]{:S(2)}) async-start(bf16[128,24,128]{2,1,0:T(8,128)(2,1)} %pad_maximum_fusion), calls=%async_computation.3 | async-start | bytes 1572864 | tf_op jit(solution)/shard_map/all_to_all | solution.py:370
  230.0 10.2 %shard_map.98 = bf16[128,512]{1,0:T(8,128)(2,1)} custom-call(bf16[4,2,32,512]{3,2,1,0:T(8,128)(2,1)} %copy-done.8, bf16[4,2,32,512]{3,2,1,0:T(8,128)(2,1)} %collective-permute-done.12.near_ref, bf16[3,3,3,512,512]{4,3,2,1,0:T(8,128)(2,1)} %taps_ref.3), custom_call_target="tpu_custom_call" | custom-call | flops 8000000000 | bytes 10000000 | tf_op jit(solution)/shard_map/pallas_call | solution.py:36
  240.2 1.7 copy.14
  241.9 4.3 %all-to-all-done.3 = bf16[128,24,128]{2,1,0:T(8,128)(2,1)S(1)} async-done(((bf16[128,24,128]{2,1,0:T(8,128)(2,1)}), bf16[128,24,128]{2,1,0:T(8,128)(2,1)S(1)}, u32[]{:S(2)}, u32[]{:S(2)}) %all-to-all-start.3) | async-done | bytes 786464 | tf_op jit(solution)/shard_map/all_to_all | solution.py:370
  247.1 3.7 %shard_map.103 = (bf16[64,2,1024]{2,1,0:T(2,128)(2,1)}, bf16[64,2,1024]{2,1,0:T(2,128)(2,1)}, bf16[64,2,1024]{2,1,0:T(2,128)(2,1)}) custom-call(bf16[4,16,2,3,8,128]{5,4,3,2,1,0:T(8,128)(2,1)} %bitcast.27), custom_call_target="tpu_custom_call" | custom-call | flops 3200000000 | bytes 4000000 | tf_op jit(solution)/shard_map/pallas_call | solution.py:36
  (72 shorter events, 16.8 us)
Async XLA Ops:
  1.6 4.4 %collective-permute-start = (bf16[1,2,32,512]{3,2,1,0:T(8,128)(2,1)S(1)}, bf16[1,2,32,512]{3,2,1,0:T(8,128)(2,1)S(1)}, u32[]{:S(2)}, u32[]{:S(2)}) collective-permute-start(bf16[1,2,32,512]{3,2,1,0:T(8,128)(2,1)S(1)} %get-tuple-element.50), channel_id=1, source_target_pairs={{0,1},{1,2},{2,3},{3,4},{4,5},{5,6},{6,7},{7,0},{8,9},{9,10},{10,1... | collective-permute-start | bytes 196616 | tf_op jit(solution)/shard_map/ppermute | solution.py:359
  4.6 3.7 %collective-permute-start.1 = (bf16[1,2,32,512]{3,2,1,0:T(8,128)(2,1)S(1)}, bf16[1,2,32,512]{3,2,1,0:T(8,128)(2,1)S(1)}, u32[]{:S(2)}, u32[]{:S(2)}) collective-permute-start(bf16[1,2,32,512]{3,2,1,0:T(8,128)(2,1)S(1)} %get-tuple-element.51), channel_id=1, source_target_pairs={{0,7},{1,0},{2,1},{3,2},{4,3},{5,4},{6,5},{7,6},{8,15},{9,8},{10,9... | collective-permute-start | bytes 196616 | tf_op jit(solution)/shard_map/ppermute | solution.py:359
  8.3 5.1 %copy-start.9 = (bf16[4,2,32,512]{3,2,1,0:T(8,128)(2,1)}, bf16[4,2,32,512]{3,2,1,0:T(8,128)(2,1)S(1)}, u32[]{:S(2)}) copy-start(bf16[4,2,32,512]{3,2,1,0:T(8,128)(2,1)S(1)} %pad_maximum_fusion.1.own_ref) | copy-start | bytes 786436
  8.3 15.7 %collective-permute-start.2 = (bf16[4,2,32,512]{3,2,1,0:T(8,128)(2,1)S(1)}, bf16[4,2,32,512]{3,2,1,0:T(8,128)(2,1)S(1)}, u32[]{:S(2)}, u32[]{:S(2)}) collective-permute-start(bf16[4,2,32,512]{3,2,1,0:T(8,128)(2,1)S(1)} %pad_maximum_fusion.1.own_ref), channel_id=1, source_target_pairs={{8,0},{16,8},{24,16},{32,24},{40,32},{48,40},{56,48},{64,56},{72,6... | collective-permute-start | bytes 786440 | tf_op jit(solution)/shard_map/ppermute | solution.py:365
  13.5 26.8 %all-to-all-start = ((bf16[128,24,128]{2,1,0:T(8,128)(2,1)}), bf16[128,24,128]{2,1,0:T(8,128)(2,1)S(1)}, u32[]{:S(2)}, u32[]{:S(2)}) async-start(bf16[128,24,128]{2,1,0:T(8,128)(2,1)} %bitcast.28), calls=%async_computation | async-start | bytes 1572864 | tf_op jit(solution)/shard_map/all_to_all | solution.py:370
  40.3 30.0 %copy-start.4 = (bf16[128,16,128]{2,1,0:T(8,128)(2,1)}, bf16[128,16,128]{2,1,0:T(8,128)(2,1)S(1)}, u32[]{:S(2)}) copy-start(bf16[128,16,128]{2,1,0:T(8,128)(2,1)S(1)} %slice.26) | copy-start | bytes 1572868
  40.3 14.2 %collective-permute-start.3 = (bf16[4,4,128,128]{3,2,1,0:T(8,128)(2,1)S(1)}, bf16[4,4,128,128]{3,2,1,0:T(8,128)(2,1)S(1)}, u32[]{:S(2)}, u32[]{:S(2)}) collective-permute-start(bf16[4,4,128,128]{3,2,1,0:T(8,128)(2,1)S(1)} %bitcast.29), channel_id=1, source_target_pairs={{0,32},{32,64},{64,96},{96,0},{1,33},{33,65},{65,97},{97,1},{2,34}... | collective-permute-start | bytes 1572872 | tf_op jit(solution)/shard_map/ppermute | solution.py:347
  40.7 29.1 %collective-permute-start.4 = (bf16[4,4,128,128]{3,2,1,0:T(8,128)(2,1)S(1)}, bf16[4,4,128,128]{3,2,1,0:T(8,128)(2,1)S(1)}, u32[]{:S(2)}, u32[]{:S(2)}) collective-permute-start(bf16[4,4,128,128]{3,2,1,0:T(8,128)(2,1)S(1)} %bitcast.30), channel_id=1, source_target_pairs={{0,96},{32,0},{64,32},{96,64},{1,97},{33,1},{65,33},{97,65},{2,98}... | collective-permute-start | bytes 1572872 | tf_op jit(solution)/shard_map/ppermute | solution.py:347
  43.1 26.8 %collective-permute-start.5 = (bf16[4,4,128,128]{3,2,1,0:T(8,128)(2,1)S(1)}, bf16[4,4,128,128]{3,2,1,0:T(8,128)(2,1)}, u32[]{:S(2)}, u32[]{:S(2)}) collective-permute-start(bf16[4,4,128,128]{3,2,1,0:T(8,128)(2,1)S(1)} %bitcast.31), channel_id=1, source_target_pairs={{0,64},{32,96},{64,0},{96,32},{1,65},{33,97},{65,1},{97,33},{2,66}... | collective-permute-start | bytes 1572872 | tf_op jit(solution)/shard_map/ppermute | solution.py:347
  43.1 27.3 %collective-permute-start.9 = (bf16[4,4,128,128]{3,2,1,0:T(8,128)(2,1)S(1)}, bf16[4,4,128,128]{3,2,1,0:T(8,128)(2,1)S(1)}, u32[]{:S(2)}, u32[]{:S(2)}) collective-permute-start(bf16[4,4,128,128]{3,2,1,0:T(8,128)(2,1)S(1)} %bitcast.32), channel_id=1, source_target_pairs={{0,1},{1,0},{2,3},{3,2},{4,5},{5,4},{6,7},{7,6},{8,9},{9,8},{10,11... | collective-permute-start | bytes 1572872 | tf_op jit(solution)/shard_map/ppermute | solution.py:351
  45.6 37.5 %all-to-all-start.1 = ((bf16[128,8,128]{2,1,0:T(8,128)(2,1)}), bf16[128,8,128]{2,1,0:T(8,128)(2,1)S(1)}, u32[]{:S(2)}, u32[]{:S(2)}) async-start(bf16[128,8,128]{2,1,0:T(8,128)(2,1)} %bitcast.6), calls=%async_computation.1 | async-start | bytes 524288 | tf_op jit(solution)/shard_map/all_to_all | solution.py:370
  54.5 28.6 %copy-start.13 = (bf16[4,4,128,128]{3,2,1,0:T(8,128)(2,1)}, bf16[4,4,128,128]{3,2,1,0:T(8,128)(2,1)S(1)}, u32[]{:S(2)}) copy-start(bf16[4,4,128,128]{3,2,1,0:T(8,128)(2,1)S(1)} %collective-permute-done.3.refs_0_.same_ref) | copy-start | bytes 1572868
  54.5 28.7 %collective-permute-start.6 = (bf16[4,4,128,128]{3,2,1,0:T(8,128)(2,1)S(1)}, bf16[4,4,128,128]{3,2,1,0:T(8,128)(2,1)}, u32[]{:S(2)}, u32[]{:S(2)}) collective-permute-start(bf16[4,4,128,128]{3,2,1,0:T(8,128)(2,1)S(1)} %collective-permute-done.3.refs_0_.same_ref), channel_id=1, source_target_pairs={{0,1},{1,0},{2,3},{3,2},{4,5},{5,4},{6,7},{7,6},{8,9},{9,8},{10,11... | collective-permute-start | bytes 1572872 | tf_op jit(solution)/shard_map/ppermute | solution.py:351
  69.8 13.3 %copy-start.12 = (bf16[4,4,128,128]{3,2,1,0:T(8,128)(2,1)}, bf16[4,4,128,128]{3,2,1,0:T(8,128)(2,1)S(1)}, u32[]{:S(2)}) copy-start(bf16[4,4,128,128]{3,2,1,0:T(8,128)(2,1)S(1)} %collective-permute-done.4.refs_1_.same_ref) | copy-start | bytes 1572868
  69.8 13.4 %collective-permute-start.7 = (bf16[4,4,128,128]{3,2,1,0:T(8,128)(2,1)S(1)}, bf16[4,4,128,128]{3,2,1,0:T(8,128)(2,1)S(1)}, u32[]{:S(2)}, u32[]{:S(2)}) collective-permute-start(bf16[4,4,128,128]{3,2,1,0:T(8,128)(2,1)S(1)} %collective-permute-done.4.refs_1_.same_ref), channel_id=1, source_target_pairs={{0,1},{1,0},{2,3},{3,2},{4,5},{5,4},{6,7},{7,6},{8,9},{9,8},{10,11... | collective-permute-start | bytes 1572872 | tf_op jit(solution)/shard_map/ppermute | solution.py:351
  69.9 13.3 %collective-permute-start.8 = (bf16[4,4,128,128]{3,2,1,0:T(8,128)(2,1)}, bf16[4,4,128,128]{3,2,1,0:T(8,128)(2,1)}, u32[]{:S(2)}, u32[]{:S(2)}) collective-permute-start(bf16[4,4,128,128]{3,2,1,0:T(8,128)(2,1)} %collective-permute-done.5.refs_2_.same_ref), channel_id=1, source_target_pairs={{0,1},{1,0},{2,3},{3,2},{4,5},{5,4},{6,7},{7,6},{8,9},{9,8},{10,11... | collective-permute-start | bytes 1572872 | tf_op jit(solution)/shard_map/ppermute | solution.py:351
  127.1 59.8 %collective-permute-start.13 = (bf16[4,4,128,128]{3,2,1,0:T(8,128)(2,1)}, bf16[4,4,128,128]{3,2,1,0:T(8,128)(2,1)S(1)}, u32[]{:S(2)}, u32[]{:S(2)}) collective-permute-start(bf16[4,4,128,128]{3,2,1,0:T(8,128)(2,1)} %get-tuple-element.38), channel_id=1, source_target_pairs={{0,1},{1,0},{2,3},{3,2},{4,5},{5,4},{6,7},{7,6},{8,9},{9,8},{10,11... | collective-permute-start | bytes 1572872 | tf_op jit(solution)/shard_map/ppermute | solution.py:351
  145.0 45.1 %collective-permute-start.15 = (bf16[4,4,128,128]{3,2,1,0:T(8,128)(2,1)}, bf16[4,4,128,128]{3,2,1,0:T(8,128)(2,1)S(1)}, u32[]{:S(2)}, u32[]{:S(2)}) collective-permute-start(bf16[4,4,128,128]{3,2,1,0:T(8,128)(2,1)} %get-tuple-element.40), channel_id=1, source_target_pairs={{0,1},{1,0},{2,3},{3,2},{4,5},{5,4},{6,7},{7,6},{8,9},{9,8},{10,11... | collective-permute-start | bytes 1572872 | tf_op jit(solution)/shard_map/ppermute | solution.py:351
  162.9 28.3 %collective-permute-start.17 = (bf16[4,4,128,128]{3,2,1,0:T(8,128)(2,1)}, bf16[4,4,128,128]{3,2,1,0:T(8,128)(2,1)S(1)}, u32[]{:S(2)}, u32[]{:S(2)}) collective-permute-start(bf16[4,4,128,128]{3,2,1,0:T(8,128)(2,1)} %get-tuple-element.42), channel_id=1, source_target_pairs={{0,1},{1,0},{2,3},{3,2},{4,5},{5,4},{6,7},{7,6},{8,9},{9,8},{10,11... | collective-permute-start | bytes 1572872 | tf_op jit(solution)/shard_map/ppermute | solution.py:351
  163.1 23.8 %copy-start.3 = (bf16[4,4,128,128]{3,2,1,0:T(8,128)(2,1)S(1)}, bf16[4,4,128,128]{3,2,1,0:T(8,128)(2,1)}, u32[]{:S(2)}) copy-start(bf16[4,4,128,128]{3,2,1,0:T(8,128)(2,1)} %get-tuple-element.37) | copy-start | bytes 1572868
  180.5 9.5 %copy-start.2 = (bf16[4,4,128,128]{3,2,1,0:T(8,128)(2,1)S(1)}, bf16[4,4,128,128]{3,2,1,0:T(8,128)(2,1)}, u32[]{:S(2)}) copy-start(bf16[4,4,128,128]{3,2,1,0:T(8,128)(2,1)} %get-tuple-element.39) | copy-start | bytes 1572868
  180.5 32.1 %collective-permute-start.19 = (bf16[4,4,128,128]{3,2,1,0:T(8,128)(2,1)}, bf16[4,4,128,128]{3,2,1,0:T(8,128)(2,1)}, u32[]{:S(2)}, u32[]{:S(2)}) collective-permute-start(bf16[4,4,128,128]{3,2,1,0:T(8,128)(2,1)} %get-tuple-element.44), channel_id=1, source_target_pairs={{0,1},{1,0},{2,3},{3,2},{4,5},{5,4},{6,7},{7,6},{8,9},{9,8},{10,11... | collective-permute-start | bytes 1572872 | tf_op jit(solution)/shard_map/ppermute | solution.py:351
  180.8 17.0 %all-to-all-start.2 = ((bf16[128,8,128]{2,1,0:T(8,128)(2,1)}), bf16[128,8,128]{2,1,0:T(8,128)(2,1)S(1)}, u32[]{:S(2)}, u32[]{:S(2)}) async-start(bf16[128,8,128]{2,1,0:T(8,128)(2,1)} %bitcast.7), calls=%async_computation.2 | async-start | bytes 524288 | tf_op jit(solution)/shard_map/all_to_all | solution.py:370
  187.1 25.5 %collective-permute-start.14 = (bf16[4,4,128,128]{3,2,1,0:T(8,128)(2,1)S(1)}, bf16[4,4,128,128]{3,2,1,0:T(8,128)(2,1)S(1)}, u32[]{:S(2)}, u32[]{:S(2)}) collective-permute-start(bf16[4,4,128,128]{3,2,1,0:T(8,128)(2,1)S(1)} %add_convert_fusion.3), channel_id=1, source_target_pairs={{0,64},{32,96},{64,0},{96,32},{1,65},{33,97},{65,1},{97,33},{2,66}... | collective-permute-start | bytes 1572872 | tf_op jit(solution)/shard_map/ppermute | solution.py:347
  190.2 25.0 %collective-permute-start.16 = (bf16[4,4,128,128]{3,2,1,0:T(8,128)(2,1)S(1)}, bf16[4,4,128,128]{3,2,1,0:T(8,128)(2,1)S(1)}, u32[]{:S(2)}, u32[]{:S(2)}) collective-permute-start(bf16[4,4,128,128]{3,2,1,0:T(8,128)(2,1)S(1)} %add_convert_fusion.2), channel_id=1, source_target_pairs={{0,96},{32,0},{64,32},{96,64},{1,97},{33,1},{65,33},{97,65},{2,98}... | collective-permute-start | bytes 1572872 | tf_op jit(solution)/shard_map/ppermute | solution.py:347
  191.3 24.8 %collective-permute-start.18 = (bf16[4,4,128,128]{3,2,1,0:T(8,128)(2,1)S(1)}, bf16[4,4,128,128]{3,2,1,0:T(8,128)(2,1)S(1)}, u32[]{:S(2)}, u32[]{:S(2)}) collective-permute-start(bf16[4,4,128,128]{3,2,1,0:T(8,128)(2,1)S(1)} %add_convert_fusion.1), channel_id=1, source_target_pairs={{0,32},{32,64},{64,96},{96,0},{1,33},{33,65},{65,97},{97,1},{2,34}... | collective-permute-start | bytes 1572872 | tf_op jit(solution)/shard_map/ppermute | solution.py:347
  198.5 17.6 %copy-start.5 = (bf16[4,4,128,128]{3,2,1,0:T(8,128)(2,1)S(1)}, bf16[4,4,128,128]{3,2,1,0:T(8,128)(2,1)}, u32[]{:S(2)}) copy-start(bf16[4,4,128,128]{3,2,1,0:T(8,128)(2,1)} %get-tuple-element.43) | copy-start | bytes 1572868
  201.8 2.3 collective-permute-start.10
  204.1 4.6 %collective-permute-start.11 = (bf16[1,2,32,512]{3,2,1,0:T(8,128)(2,1)S(1)}, bf16[1,2,32,512]{3,2,1,0:T(8,128)(2,1)S(1)}, u32[]{:S(2)}, u32[]{:S(2)}) collective-permute-start(bf16[1,2,32,512]{3,2,1,0:T(8,128)(2,1)S(1)} %bitcast.40), channel_id=1, source_target_pairs={{0,7},{1,0},{2,1},{3,2},{4,3},{5,4},{6,5},{7,6},{8,15},{9,8},{10,9... | collective-permute-start | bytes 196616 | tf_op jit(solution)/shard_map/ppermute | solution.py:359
  209.6 7.9 %copy-start.8 = (bf16[4,2,32,512]{3,2,1,0:T(8,128)(2,1)}, bf16[4,2,32,512]{3,2,1,0:T(8,128)(2,1)S(1)}, u32[]{:S(2)}) copy-start(bf16[4,2,32,512]{3,2,1,0:T(8,128)(2,1)S(1)} %pad_maximum_fusion.2.own_ref) | copy-start | bytes 786436
  209.6 20.3 %collective-permute-start.12 = (bf16[4,2,32,512]{3,2,1,0:T(8,128)(2,1)S(1)}, bf16[4,2,32,512]{3,2,1,0:T(8,128)(2,1)}, u32[]{:S(2)}, u32[]{:S(2)}) collective-permute-start(bf16[4,2,32,512]{3,2,1,0:T(8,128)(2,1)S(1)} %pad_maximum_fusion.2.own_ref), channel_id=1, source_target_pairs={{0,8},{8,16},{16,24},{24,32},{32,40},{40,48},{48,56},{56,64},{64,7... | collective-permute-start | bytes 786440 | tf_op jit(solution)/shard_map/ppermute | solution.py:365
  218.6 27.7 %all-to-all-start.3 = ((bf16[128,24,128]{2,1,0:T(8,128)(2,1)}), bf16[128,24,128]{2,1,0:T(8,128)(2,1)S(1)}, u32[]{:S(2)}, u32[]{:S(2)}) async-start(bf16[128,24,128]{2,1,0:T(8,128)(2,1)} %pad_maximum_fusion), calls=%async_computation.3 | async-start | bytes 1572864 | tf_op jit(solution)/shard_map/all_to_all | solution.py:370
  (8 other events, 10.5 us)

commit v2 on v1

--- a/solution.py
+++ b/solution.py
@@ -266,15 +266,17 @@
             return 0
 
         lax.fori_loop(0, block, whole, 0)
-        for half in range(2):
-            count = TOK - 256 * half
-            query = query_ref[pl.ds(pl.multiple_of(start + half * 256, 256), count), :]
-            keys = kv_ref[block, 2 * half : 2 * half + 2].reshape(number * 256, 128)
+        width = 128 if number == 2 else 256
+        for part in range(TOK // width):
+            count = TOK - width * part
+            query = query_ref[pl.ds(pl.multiple_of(start + part * width, width), count), :]
+            each = width // 128
+            keys = kv_ref[block, each * part : each * (part + 1)].reshape(number * width, 128)
             row = lax.broadcasted_iota(jnp.int32, (count, 1), 0)
-            key = lax.broadcasted_iota(jnp.int32, (1, number * 256), 1)
+            key = lax.broadcasted_iota(jnp.int32, (1, number * width), 1)
             hidden = row // 128 * 2 + row % 2 < key // (number * 128) * 2 + key % 2
             scores = jnp.where(hidden, NEGATIVE, dot(query, keys, NT))
-            update(slice(half * 256, TOK), scores, keys)
+            update(slice(part * width, TOK), scores, keys)
         acc = acc_ref[...]
         if not last:
             state_ref[rows, :] = jnp.where(lane == 1, max_ref[...], acc)
@@ -411,7 +413,6 @@
         us=12.0,
     )
     packed, grad = lax.optimization_barrier((packed, grad))
-    source = packed[:, :8]
     kv_same = {0: packed[:, 8:].reshape(grouped)}
     for steps in (1, 3, 2):
         kv_same[steps] = shift_y(kv_same[0], steps)
@@ -420,6 +421,9 @@
 
     def attend(arrays, extra, outs, us, first=False, last=False):
         number = len(arrays)
+        specs = {index: pl.BlockSpec(memory_space=pl.ANY) for index in range(number)}
+        if first:
+            specs[number] = pl.BlockSpec((128, 8, 128), lambda *_: (0, 0, 0))
         return kernel_call(
             functools.partial(forward_body, number, first, last),
             outs,
@@ -430,13 +434,13 @@
                 pltpu.SemaphoreType.DMA((number,)),
             ],
             (*arrays, *extra),
-            specs={index: pl.BlockSpec(memory_space=pl.ANY) for index in range(number)},
+            specs=specs,
             us=us,
         )
 
     state = struct((SPAN, 128), F32)
     query, seed = attend(
-        [kv_same[0], kv_other[0]], (source,), [struct((SPAN, 128)), state], 10.0, True
+        [kv_same[0], kv_other[0]], (packed,), [struct((SPAN, 128)), state], 10.0, True
     )
     rest = [kv_same[i] for i in (1, 3, 2)] + [kv_other[i] for i in (1, 3, 2)]
     att, stats, grad = attend(

time: 252 us -> 251 us (level)
  no operation moved by 1% of the time
where the time goes in v2:
time: 251 us; the launch traced here: 250 us
  Pallas kernels  140 us (56%)
  starting transfers between devices  71.9 us (29%)
  waiting for transfers between devices  26.3 us (10%)
  local copies, waits for them, and re-layouts  7.34 us (3%)
  other arithmetic  3.88 us (2%)
    pallas_call x11, Pallas kernels, kernel_call(): pl.pallas_call(body, out_shape=outs, grid=grid, in_specs=in_specs, out_sp...  140 us
    all_to_all x4, starting transfers between devices, exchange_all(): return lax.all_to_all(split, AXES, split_axis=0, concat_axis=0, tiled=True)  34 us
    ppermute x8, starting transfers between devices, swap_core(): return lax.ppermute(value, 'c', [(0, 1), (1, 0)])  18.7 us
    all_to_all x4, waiting for transfers between devices, exchange_all(): return lax.all_to_all(split, AXES, split_axis=0, concat_axis=0, tiled=True)  13.2 us
    ppermute x4, starting transfers between devices, turn(): return lax.ppermute(value, ('z', 'c'), pairs)  7.7 us
    ppermute x6, starting transfers between devices, shift_y(): return lax.ppermute(value, 'y', [(i, (i + steps) % 4) for i in range(4)])  7.29 us
    ppermute x6, waiting for transfers between devices, shift_y(): return lax.ppermute(value, 'y', [(i, (i + steps) % 4) for i in range(4)])  7.12 us
    ppermute x4, waiting for transfers between devices, turn(): return lax.ppermute(value, ('z', 'c'), pairs)  5.92 us
  transfers between devices with their start and end apart: 24, of which 10 were waited for; matrix products, arithmetic and copies ran while one was open for 3% of the time, Pallas kernels for 37%

profile of v2, /device:TPU:1, one launch (start us, length us, event | category | flops | bytes accessed | tf_op | source)
XLA Modules:
  0.0 249.9 jit_solution(11127115711545381016)
XLA Ops:
  1.6 3.0 %collective-permute-start = (bf16[1,2,32,512]{3,2,1,0:T(8,128)(2,1)S(1)}, bf16[1,2,32,512]{3,2,1,0:T(8,128)(2,1)S(1)}, u32[]{:S(2)}, u32[]{:S(2)}) collective-permute-start(bf16[1,2,32,512]{3,2,1,0:T(8,128)(2,1)S(1)} %get-tuple-element.50), channel_id=1, source_target_pairs={{0,1},{1,2},{2,3},{3,4},{4,5},{5,6},{6,7},{7,0},{8,9},{9,10},{10,1... | collective-permute-start | bytes 196616 | tf_op jit(solution)/shard_map/ppermute | solution.py:361
  4.6 1.3 collective-permute-done
  5.9 2.4 collective-permute-done.1
  9.6 3.8 %shard_map.93 = bf16[4,16,2,3,8,128]{5,4,3,2,1,0:T(8,128)(2,1)} custom-call(bf16[64,2,1024]{2,1,0:T(2,128)(2,1)} %bitcast.43, bf16[64,2,1024]{2,1,0:T(2,128)(2,1)} %bitcast.44, bf16[64,2,1024]{2,1,0:T(2,128)(2,1)} %bitcast.45), custom_call_target="tpu_custom_call" | custom-call | flops 3200000000 | bytes 4000000 | tf_op jit(solution)/shard_map/pallas_call | solution.py:36
  13.5 10.6 %all-to-all-start = ((bf16[128,24,128]{2,1,0:T(8,128)(2,1)}), bf16[128,24,128]{2,1,0:T(8,128)(2,1)S(1)}, u32[]{:S(2)}, u32[]{:S(2)}) async-start(bf16[128,24,128]{2,1,0:T(8,128)(2,1)} %bitcast.28), calls=%async_computation | async-start | bytes 1572864 | tf_op jit(solution)/shard_map/all_to_all | solution.py:372
  24.7 12.4 %shard_map.94 = bf16[4,16,2,1,8,128]{5,4,3,2,1,0:T(8,128)(2,1)} custom-call(bf16[4,2,32,512]{3,2,1,0:T(8,128)(2,1)} %copy-done.10, bf16[4,2,32,512]{3,2,1,0:T(8,128)(2,1)} %copy-done.15, bf16[3,3,3,512,512]{4,3,2,1,0:T(8,128)(2,1)} %taps_ref.3, bf16[1024,512]{1,0:T(8,128)(2,1)} %proj_ref.3), custom_call_target="tpu_custom_call" | custom-call | flops 9600000000 | bytes 12000000 | tf_op jit(solution)/shard_map/pallas_call | solution.py:36
  37.2 3.1 %all-to-all-done.refs_2_ = bf16[128,24,128]{2,1,0:T(8,128)(2,1)S(1)} async-done(((bf16[128,24,128]{2,1,0:T(8,128)(2,1)}), bf16[128,24,128]{2,1,0:T(8,128)(2,1)S(1)}, u32[]{:S(2)}, u32[]{:S(2)}) %all-to-all-start) | async-done | bytes 786464 | tf_op jit(solution)/shard_map/all_to_all | solution.py:372
  40.7 2.3 collective-permute-start.4
  43.1 1.9 collective-permute-start.9
  44.9 5.9 %all-to-all-start.1 = ((bf16[128,8,128]{2,1,0:T(8,128)(2,1)}), bf16[128,8,128]{2,1,0:T(8,128)(2,1)S(1)}, u32[]{:S(2)}, u32[]{:S(2)}) async-start(bf16[128,8,128]{2,1,0:T(8,128)(2,1)} %bitcast.36), calls=%async_computation.1 | async-start | bytes 524288 | tf_op jit(solution)/shard_map/all_to_all | solution.py:372
  50.9 3.6 %collective-permute-done.3.refs_0_.same_ref = bf16[4,4,128,128]{3,2,1,0:T(8,128)(2,1)S(1)} collective-permute-done((bf16[4,4,128,128]{3,2,1,0:T(8,128)(2,1)S(1)}, bf16[4,4,128,128]{3,2,1,0:T(8,128)(2,1)S(1)}, u32[]{:S(2)}, u32[]{:S(2)}) %collective-permute-start.3) | collective-permute-done | bytes 524320 | tf_op jit(solution)/shard_map/ppermute | solution.py:349
  54.5 15.3 %collective-permute-start.6 = (bf16[4,4,128,128]{3,2,1,0:T(8,128)(2,1)S(1)}, bf16[4,4,128,128]{3,2,1,0:T(8,128)(2,1)}, u32[]{:S(2)}, u32[]{:S(2)}) collective-permute-start(bf16[4,4,128,128]{3,2,1,0:T(8,128)(2,1)S(1)} %collective-permute-done.3.refs_0_.same_ref), channel_id=1, source_target_pairs={{0,1},{1,0},{2,3},{3,2},{4,5},{5,4},{6,7},{7,6},{8,9},{9,8},{10,11... | collective-permute-start | bytes 1572872 | tf_op jit(solution)/shard_map/ppermute | solution.py:353
  71.1 11.3 %shard_map.95 = (bf16[2048,128]{1,0:T(8,128)(2,1)}, f32[2048,128]{1,0:T(8,128)}) custom-call(bf16[4,4,128,128]{3,2,1,0:T(8,128)(2,1)} %bitcast.33, bf16[4,4,128,128]{3,2,1,0:T(8,128)(2,1)} %copy-done.12, bf16[128,24,128]{2,1,0:T(8,128)(2,1)} %copy-done), custom_call_target="tpu_custom_call" | custom-call | flops 8000000000 | bytes 10000000 | tf_op jit(solution)/shard_map/pallas_call | solution.py:36
  83.2 25.7 %shard_map.96 = (bf16[1024,128]{1,0:T(8,128)(2,1)}, f32[8,2048]{1,0:T(8,128)}, bf16[2048,128]{1,0:T(8,128)(2,1)}) custom-call(bf16[4,4,128,128]{3,2,1,0:T(8,128)(2,1)} %copy-done.14, bf16[4,4,128,128]{3,2,1,0:T(8,128)(2,1)} %copy-done.13, bf16[4,4,128,128]{3,2,1,0:T(8,128)(2,1)} %collective-permute-done.5.refs_2_.same_ref, ...), custom_call_target="tpu_custom_call" | custom-call | flops 20000000000 | bytes 25000000 | tf_op jit(solution)/shard_map/pallas_call | solution.py:36
  108.9 17.2 %shard_map.99 = (bf16[4,4,128,128]{3,2,1,0:T(8,128)(2,1)}, bf16[4,4,128,128]{3,2,1,0:T(8,128)(2,1)}, f32[128,2048]{1,0:T(8,128)}) custom-call(bf16[4,4,128,128]{3,2,1,0:T(8,128)(2,1)} %collective-permute-done.5.refs_2_.same_ref, bf16[4,4,128,128]{3,2,1,0:T(8,128)(2,1)} %collective-permute-done.8.refs_5_.other_ref, ...), custom_call_target="tpu_custom_call" | custom-call | flops 12800000000 | bytes 16000000 | tf_op jit(solution)/shard_map/pallas_call | solution.py:36
  126.5 17.6 %shard_map.100 = (bf16[4,4,128,128]{3,2,1,0:T(8,128)(2,1)}, bf16[4,4,128,128]{3,2,1,0:T(8,128)(2,1)}, f32[128,2048]{1,0:T(8,128)}) custom-call(bf16[4,4,128,128]{3,2,1,0:T(8,128)(2,1)} %copy-done.14, bf16[4,4,128,128]{3,2,1,0:T(8,128)(2,1)} %collective-permute-done.6.refs_3_.other_ref, bf16[2048,128]{1,0:T(8,128)(2,1)} %get-tuple-element.27.refs_6_.query_ref, ...), custom_call_target="tpu_custom_call" | custom-call | flops 12800000000 | bytes 16000000 | tf_op jit(solution)/shard_map/pallas_call | solution.py:36
  144.3 17.7 %shard_map.101 = (bf16[4,4,128,128]{3,2,1,0:T(8,128)(2,1)}, bf16[4,4,128,128]{3,2,1,0:T(8,128)(2,1)}, f32[128,2048]{1,0:T(8,128)}) custom-call(bf16[4,4,128,128]{3,2,1,0:T(8,128)(2,1)} %copy-done.13, bf16[4,4,128,128]{3,2,1,0:T(8,128)(2,1)} %collective-permute-done.7.refs_4_.other_ref, bf16[2048,128]{1,0:T(8,128)(2,1)} %get-tuple-element.27.refs_6_.query_ref, ...), custom_call_target="tpu_custom_call" | custom-call | flops 12800000000 | bytes 16000000 | tf_op jit(solution)/shard_map/pallas_call | solution.py:36
  162.3 17.4 %shard_map.102 = (bf16[4,4,128,128]{3,2,1,0:T(8,128)(2,1)}, bf16[4,4,128,128]{3,2,1,0:T(8,128)(2,1)}, bf16[1024,128]{1,0:T(8,128)(2,1)}) custom-call(bf16[4,4,128,128]{3,2,1,0:T(8,128)(2,1)} %bitcast.34, bf16[4,4,128,128]{3,2,1,0:T(8,128)(2,1)} %copy-done.12, bf16[2048,128]{1,0:T(8,128)(2,1)} %get-tuple-element.27.refs_6_.query_ref, ...), custom_call_target="tpu_custom_call" | custom-call | flops 12800000000 | bytes 16000000 | tf_op jit(solution)/shard_map/pallas_call | solution.py:36
  179.9 6.1 %all-to-all-start.2 = ((bf16[128,8,128]{2,1,0:T(8,128)(2,1)}), bf16[128,8,128]{2,1,0:T(8,128)(2,1)S(1)}, u32[]{:S(2)}, u32[]{:S(2)}) async-start(bf16[128,8,128]{2,1,0:T(8,128)(2,1)} %bitcast.7), calls=%async_computation.2 | async-start | bytes 524288 | tf_op jit(solution)/shard_map/all_to_all | solution.py:372
  186.2 2.9 %collective-permute-start.14 = (bf16[4,4,128,128]{3,2,1,0:T(8,128)(2,1)S(1)}, bf16[4,4,128,128]{3,2,1,0:T(8,128)(2,1)S(1)}, u32[]{:S(2)}, u32[]{:S(2)}) collective-permute-start(bf16[4,4,128,128]{3,2,1,0:T(8,128)(2,1)S(1)} %add_convert_fusion.3), channel_id=1, source_target_pairs={{0,64},{32,96},{64,0},{96,32},{1,65},{33,97},{65,1},{97,33},{2,66}... | collective-permute-start | bytes 1572872 | tf_op jit(solution)/shard_map/ppermute | solution.py:349
  191.1 5.9 %all-to-all-done.2 = bf16[128,8,128]{2,1,0:T(8,128)(2,1)S(1)} async-done(((bf16[128,8,128]{2,1,0:T(8,128)(2,1)}), bf16[128,8,128]{2,1,0:T(8,128)(2,1)S(1)}, u32[]{:S(2)}, u32[]{:S(2)}) %all-to-all-start.2) | async-done | bytes 262176 | tf_op jit(solution)/shard_map/all_to_all | solution.py:372
  197.6 2.4 shard_map.97
  201.9 1.3 collective-permute-done.10
  203.2 3.7 %collective-permute-start.11 = (bf16[1,2,32,512]{3,2,1,0:T(8,128)(2,1)S(1)}, bf16[1,2,32,512]{3,2,1,0:T(8,128)(2,1)S(1)}, u32[]{:S(2)}, u32[]{:S(2)}) collective-permute-start(bf16[1,2,32,512]{3,2,1,0:T(8,128)(2,1)S(1)} %bitcast.41), channel_id=1, source_target_pairs={{0,7},{1,0},{2,1},{3,2},{4,3},{5,4},{6,5},{7,6},{8,15},{9,8},{10,9... | collective-permute-start | bytes 196616 | tf_op jit(solution)/shard_map/ppermute | solution.py:361
  208.8 2.9 %collective-permute-start.12 = (bf16[4,2,32,512]{3,2,1,0:T(8,128)(2,1)S(1)}, bf16[4,2,32,512]{3,2,1,0:T(8,128)(2,1)}, u32[]{:S(2)}, u32[]{:S(2)}) collective-permute-start(bf16[4,2,32,512]{3,2,1,0:T(8,128)(2,1)S(1)} %pad_maximum_fusion.2.own_ref), channel_id=1, source_target_pairs={{0,8},{8,16},{16,24},{24,32},{32,40},{40,48},{48,56},{56,64},{64,7... | collective-permute-start | bytes 786440 | tf_op jit(solution)/shard_map/ppermute | solution.py:367
  211.7 2.6 %collective-permute-done.16 = bf16[4,4,128,128]{3,2,1,0:T(8,128)(2,1)S(1)} collective-permute-done((bf16[4,4,128,128]{3,2,1,0:T(8,128)(2,1)S(1)}, bf16[4,4,128,128]{3,2,1,0:T(8,128)(2,1)S(1)}, u32[]{:S(2)}, u32[]{:S(2)}) %collective-permute-start.16) | collective-permute-done | bytes 524320 | tf_op jit(solution)/shard_map/ppermute | solution.py:349
  215.2 1.5 add_convert_fusion
  217.7 11.4 %all-to-all-start.3 = ((bf16[128,24,128]{2,1,0:T(8,128)(2,1)}), bf16[128,24,128]{2,1,0:T(8,128)(2,1)S(1)}, u32[]{:S(2)}, u32[]{:S(2)}) async-start(bf16[128,24,128]{2,1,0:T(8,128)(2,1)} %pad_maximum_fusion), calls=%async_computation.3 | async-start | bytes 1572864 | tf_op jit(solution)/shard_map/all_to_all | solution.py:372
  229.1 10.2 %shard_map.98 = bf16[128,512]{1,0:T(8,128)(2,1)} custom-call(bf16[4,2,32,512]{3,2,1,0:T(8,128)(2,1)} %copy-done.9, bf16[4,2,32,512]{3,2,1,0:T(8,128)(2,1)} %collective-permute-done.12.near_ref, bf16[3,3,3,512,512]{4,3,2,1,0:T(8,128)(2,1)} %taps_ref.3), custom_call_target="tpu_custom_call" | custom-call | flops 8000000000 | bytes 10000000 | tf_op jit(solution)/shard_map/pallas_call | solution.py:36
  239.4 1.7 copy.14
  241.1 4.3 %all-to-all-done.3 = bf16[128,24,128]{2,1,0:T(8,128)(2,1)S(1)} async-done(((bf16[128,24,128]{2,1,0:T(8,128)(2,1)}), bf16[128,24,128]{2,1,0:T(8,128)(2,1)S(1)}, u32[]{:S(2)}, u32[]{:S(2)}) %all-to-all-start.3) | async-done | bytes 786464 | tf_op jit(solution)/shard_map/all_to_all | solution.py:372
  246.3 3.7 %shard_map.103 = (bf16[64,2,1024]{2,1,0:T(2,128)(2,1)}, bf16[64,2,1024]{2,1,0:T(2,128)(2,1)}, bf16[64,2,1024]{2,1,0:T(2,128)(2,1)}) custom-call(bf16[4,16,2,3,8,128]{5,4,3,2,1,0:T(8,128)(2,1)} %bitcast.27), custom_call_target="tpu_custom_call" | custom-call | flops 3200000000 | bytes 4000000 | tf_op jit(solution)/shard_map/pallas_call | solution.py:36
  (71 shorter events, 15.6 us)
Async XLA Ops:
  1.6 4.4 %collective-permute-start = (bf16[1,2,32,512]{3,2,1,0:T(8,128)(2,1)S(1)}, bf16[1,2,32,512]{3,2,1,0:T(8,128)(2,1)S(1)}, u32[]{:S(2)}, u32[]{:S(2)}) collective-permute-start(bf16[1,2,32,512]{3,2,1,0:T(8,128)(2,1)S(1)} %get-tuple-element.50), channel_id=1, source_target_pairs={{0,1},{1,2},{2,3},{3,4},{4,5},{5,6},{6,7},{7,0},{8,9},{9,10},{10,1... | collective-permute-start | bytes 196616 | tf_op jit(solution)/shard_map/ppermute | solution.py:361
  4.6 3.7 %collective-permute-start.1 = (bf16[1,2,32,512]{3,2,1,0:T(8,128)(2,1)S(1)}, bf16[1,2,32,512]{3,2,1,0:T(8,128)(2,1)S(1)}, u32[]{:S(2)}, u32[]{:S(2)}) collective-permute-start(bf16[1,2,32,512]{3,2,1,0:T(8,128)(2,1)S(1)} %get-tuple-element.51), channel_id=1, source_target_pairs={{0,7},{1,0},{2,1},{3,2},{4,3},{5,4},{6,5},{7,6},{8,15},{9,8},{10,9... | collective-permute-start | bytes 196616 | tf_op jit(solution)/shard_map/ppermute | solution.py:361
  8.3 15.7 %collective-permute-start.2 = (bf16[4,2,32,512]{3,2,1,0:T(8,128)(2,1)S(1)}, bf16[4,2,32,512]{3,2,1,0:T(8,128)(2,1)S(1)}, u32[]{:S(2)}, u32[]{:S(2)}) collective-permute-start(bf16[4,2,32,512]{3,2,1,0:T(8,128)(2,1)S(1)} %pad_maximum_fusion.1.own_ref), channel_id=1, source_target_pairs={{8,0},{16,8},{24,16},{32,24},{40,32},{48,40},{56,48},{64,56},{72,6... | collective-permute-start | bytes 786440 | tf_op jit(solution)/shard_map/ppermute | solution.py:367
  13.5 26.8 %all-to-all-start = ((bf16[128,24,128]{2,1,0:T(8,128)(2,1)}), bf16[128,24,128]{2,1,0:T(8,128)(2,1)S(1)}, u32[]{:S(2)}, u32[]{:S(2)}) async-start(bf16[128,24,128]{2,1,0:T(8,128)(2,1)} %bitcast.28), calls=%async_computation | async-start | bytes 1572864 | tf_op jit(solution)/shard_map/all_to_all | solution.py:372
  40.3 30.1 %copy-start = (bf16[128,24,128]{2,1,0:T(8,128)(2,1)}, bf16[128,24,128]{2,1,0:T(8,128)(2,1)S(1)}, u32[]{:S(2)}) copy-start(bf16[128,24,128]{2,1,0:T(8,128)(2,1)S(1)} %all-to-all-done.refs_2_) | copy-start | bytes 2359300
  40.3 30.0 %copy-start.5 = (bf16[128,16,128]{2,1,0:T(8,128)(2,1)}, bf16[128,16,128]{2,1,0:T(8,128)(2,1)S(1)}, u32[]{:S(2)}) copy-start(bf16[128,16,128]{2,1,0:T(8,128)(2,1)S(1)} %slice.23) | copy-start | bytes 1572868
  40.3 14.2 %collective-permute-start.3 = (bf16[4,4,128,128]{3,2,1,0:T(8,128)(2,1)S(1)}, bf16[4,4,128,128]{3,2,1,0:T(8,128)(2,1)S(1)}, u32[]{:S(2)}, u32[]{:S(2)}) collective-permute-start(bf16[4,4,128,128]{3,2,1,0:T(8,128)(2,1)S(1)} %bitcast.29), channel_id=1, source_target_pairs={{0,32},{32,64},{64,96},{96,0},{1,33},{33,65},{65,97},{97,1},{2,34}... | collective-permute-start | bytes 1572872 | tf_op jit(solution)/shard_map/ppermute | solution.py:349
  40.7 29.1 %collective-permute-start.4 = (bf16[4,4,128,128]{3,2,1,0:T(8,128)(2,1)S(1)}, bf16[4,4,128,128]{3,2,1,0:T(8,128)(2,1)S(1)}, u32[]{:S(2)}, u32[]{:S(2)}) collective-permute-start(bf16[4,4,128,128]{3,2,1,0:T(8,128)(2,1)S(1)} %bitcast.30), channel_id=1, source_target_pairs={{0,96},{32,0},{64,32},{96,64},{1,97},{33,1},{65,33},{97,65},{2,98}... | collective-permute-start | bytes 1572872 | tf_op jit(solution)/shard_map/ppermute | solution.py:349
  43.1 26.8 %collective-permute-start.5 = (bf16[4,4,128,128]{3,2,1,0:T(8,128)(2,1)S(1)}, bf16[4,4,128,128]{3,2,1,0:T(8,128)(2,1)}, u32[]{:S(2)}, u32[]{:S(2)}) collective-permute-start(bf16[4,4,128,128]{3,2,1,0:T(8,128)(2,1)S(1)} %bitcast.31), channel_id=1, source_target_pairs={{0,64},{32,96},{64,0},{96,32},{1,65},{33,97},{65,1},{97,33},{2,66}... | collective-permute-start | bytes 1572872 | tf_op jit(solution)/shard_map/ppermute | solution.py:349
  43.1 27.3 %collective-permute-start.9 = (bf16[4,4,128,128]{3,2,1,0:T(8,128)(2,1)S(1)}, bf16[4,4,128,128]{3,2,1,0:T(8,128)(2,1)S(1)}, u32[]{:S(2)}, u32[]{:S(2)}) collective-permute-start(bf16[4,4,128,128]{3,2,1,0:T(8,128)(2,1)S(1)} %bitcast.32), channel_id=1, source_target_pairs={{0,1},{1,0},{2,3},{3,2},{4,5},{5,4},{6,7},{7,6},{8,9},{9,8},{10,11... | collective-permute-start | bytes 1572872 | tf_op jit(solution)/shard_map/ppermute | solution.py:353
  44.9 37.5 %all-to-all-start.1 = ((bf16[128,8,128]{2,1,0:T(8,128)(2,1)}), bf16[128,8,128]{2,1,0:T(8,128)(2,1)S(1)}, u32[]{:S(2)}, u32[]{:S(2)}) async-start(bf16[128,8,128]{2,1,0:T(8,128)(2,1)} %bitcast.36), calls=%async_computation.1 | async-start | bytes 524288 | tf_op jit(solution)/shard_map/all_to_all | solution.py:372
  54.5 28.0 %copy-start.14 = (bf16[4,4,128,128]{3,2,1,0:T(8,128)(2,1)}, bf16[4,4,128,128]{3,2,1,0:T(8,128)(2,1)S(1)}, u32[]{:S(2)}) copy-start(bf16[4,4,128,128]{3,2,1,0:T(8,128)(2,1)S(1)} %collective-permute-done.3.refs_0_.same_ref) | copy-start | bytes 1572868
  54.5 28.0 %collective-permute-start.6 = (bf16[4,4,128,128]{3,2,1,0:T(8,128)(2,1)S(1)}, bf16[4,4,128,128]{3,2,1,0:T(8,128)(2,1)}, u32[]{:S(2)}, u32[]{:S(2)}) collective-permute-start(bf16[4,4,128,128]{3,2,1,0:T(8,128)(2,1)S(1)} %collective-permute-done.3.refs_0_.same_ref), channel_id=1, source_target_pairs={{0,1},{1,0},{2,3},{3,2},{4,5},{5,4},{6,7},{7,6},{8,9},{9,8},{10,11... | collective-permute-start | bytes 1572872 | tf_op jit(solution)/shard_map/ppermute | solution.py:353
  69.8 12.7 %copy-start.13 = (bf16[4,4,128,128]{3,2,1,0:T(8,128)(2,1)}, bf16[4,4,128,128]{3,2,1,0:T(8,128)(2,1)S(1)}, u32[]{:S(2)}) copy-start(bf16[4,4,128,128]{3,2,1,0:T(8,128)(2,1)S(1)} %collective-permute-done.4.refs_1_.same_ref) | copy-start | bytes 1572868
  69.8 12.7 %collective-permute-start.7 = (bf16[4,4,128,128]{3,2,1,0:T(8,128)(2,1)S(1)}, bf16[4,4,128,128]{3,2,1,0:T(8,128)(2,1)}, u32[]{:S(2)}, u32[]{:S(2)}) collective-permute-start(bf16[4,4,128,128]{3,2,1,0:T(8,128)(2,1)S(1)} %collective-permute-done.4.refs_1_.same_ref), channel_id=1, source_target_pairs={{0,1},{1,0},{2,3},{3,2},{4,5},{5,4},{6,7},{7,6},{8,9},{9,8},{10,11... | collective-permute-start | bytes 1572872 | tf_op jit(solution)/shard_map/ppermute | solution.py:353
  69.9 12.6 %collective-permute-start.8 = (bf16[4,4,128,128]{3,2,1,0:T(8,128)(2,1)}, bf16[4,4,128,128]{3,2,1,0:T(8,128)(2,1)}, u32[]{:S(2)}, u32[]{:S(2)}) collective-permute-start(bf16[4,4,128,128]{3,2,1,0:T(8,128)(2,1)} %collective-permute-done.5.refs_2_.same_ref), channel_id=1, source_target_pairs={{0,1},{1,0},{2,3},{3,2},{4,5},{5,4},{6,7},{7,6},{8,9},{9,8},{10,11... | collective-permute-start | bytes 1572872 | tf_op jit(solution)/shard_map/ppermute | solution.py:353
  126.2 59.9 %collective-permute-start.13 = (bf16[4,4,128,128]{3,2,1,0:T(8,128)(2,1)}, bf16[4,4,128,128]{3,2,1,0:T(8,128)(2,1)S(1)}, u32[]{:S(2)}, u32[]{:S(2)}) collective-permute-start(bf16[4,4,128,128]{3,2,1,0:T(8,128)(2,1)} %get-tuple-element.38), channel_id=1, source_target_pairs={{0,1},{1,0},{2,3},{3,2},{4,5},{5,4},{6,7},{7,6},{8,9},{9,8},{10,11... | collective-permute-start | bytes 1572872 | tf_op jit(solution)/shard_map/ppermute | solution.py:353
  144.1 45.1 %collective-permute-start.15 = (bf16[4,4,128,128]{3,2,1,0:T(8,128)(2,1)}, bf16[4,4,128,128]{3,2,1,0:T(8,128)(2,1)S(1)}, u32[]{:S(2)}, u32[]{:S(2)}) collective-permute-start(bf16[4,4,128,128]{3,2,1,0:T(8,128)(2,1)} %get-tuple-element.40), channel_id=1, source_target_pairs={{0,1},{1,0},{2,3},{3,2},{4,5},{5,4},{6,7},{7,6},{8,9},{9,8},{10,11... | collective-permute-start | bytes 1572872 | tf_op jit(solution)/shard_map/ppermute | solution.py:353
  162.0 28.3 %collective-permute-start.17 = (bf16[4,4,128,128]{3,2,1,0:T(8,128)(2,1)}, bf16[4,4,128,128]{3,2,1,0:T(8,128)(2,1)S(1)}, u32[]{:S(2)}, u32[]{:S(2)}) collective-permute-start(bf16[4,4,128,128]{3,2,1,0:T(8,128)(2,1)} %get-tuple-element.42), channel_id=1, source_target_pairs={{0,1},{1,0},{2,3},{3,2},{4,5},{5,4},{6,7},{7,6},{8,9},{9,8},{10,11... | collective-permute-start | bytes 1572872 | tf_op jit(solution)/shard_map/ppermute | solution.py:353
  162.3 23.8 %copy-start.4 = (bf16[4,4,128,128]{3,2,1,0:T(8,128)(2,1)S(1)}, bf16[4,4,128,128]{3,2,1,0:T(8,128)(2,1)}, u32[]{:S(2)}) copy-start(bf16[4,4,128,128]{3,2,1,0:T(8,128)(2,1)} %get-tuple-element.37) | copy-start | bytes 1572868
  179.7 9.5 %copy-start.3 = (bf16[4,4,128,128]{3,2,1,0:T(8,128)(2,1)S(1)}, bf16[4,4,128,128]{3,2,1,0:T(8,128)(2,1)}, u32[]{:S(2)}) copy-start(bf16[4,4,128,128]{3,2,1,0:T(8,128)(2,1)} %get-tuple-element.39) | copy-start | bytes 1572868
  179.7 32.1 %collective-permute-start.19 = (bf16[4,4,128,128]{3,2,1,0:T(8,128)(2,1)}, bf16[4,4,128,128]{3,2,1,0:T(8,128)(2,1)}, u32[]{:S(2)}, u32[]{:S(2)}) collective-permute-start(bf16[4,4,128,128]{3,2,1,0:T(8,128)(2,1)} %get-tuple-element.44), channel_id=1, source_target_pairs={{0,1},{1,0},{2,3},{3,2},{4,5},{5,4},{6,7},{7,6},{8,9},{9,8},{10,11... | collective-permute-start | bytes 1572872 | tf_op jit(solution)/shard_map/ppermute | solution.py:353
  179.9 17.0 %all-to-all-start.2 = ((bf16[128,8,128]{2,1,0:T(8,128)(2,1)}), bf16[128,8,128]{2,1,0:T(8,128)(2,1)S(1)}, u32[]{:S(2)}, u32[]{:S(2)}) async-start(bf16[128,8,128]{2,1,0:T(8,128)(2,1)} %bitcast.7), calls=%async_computation.2 | async-start | bytes 524288 | tf_op jit(solution)/shard_map/all_to_all | solution.py:372
  186.2 25.5 %collective-permute-start.14 = (bf16[4,4,128,128]{3,2,1,0:T(8,128)(2,1)S(1)}, bf16[4,4,128,128]{3,2,1,0:T(8,128)(2,1)S(1)}, u32[]{:S(2)}, u32[]{:S(2)}) collective-permute-start(bf16[4,4,128,128]{3,2,1,0:T(8,128)(2,1)S(1)} %add_convert_fusion.3), channel_id=1, source_target_pairs={{0,64},{32,96},{64,0},{96,32},{1,65},{33,97},{65,1},{97,33},{2,66}... | collective-permute-start | bytes 1572872 | tf_op jit(solution)/shard_map/ppermute | solution.py:349
  189.3 25.0 %collective-permute-start.16 = (bf16[4,4,128,128]{3,2,1,0:T(8,128)(2,1)S(1)}, bf16[4,4,128,128]{3,2,1,0:T(8,128)(2,1)S(1)}, u32[]{:S(2)}, u32[]{:S(2)}) collective-permute-start(bf16[4,4,128,128]{3,2,1,0:T(8,128)(2,1)S(1)} %add_convert_fusion.2), channel_id=1, source_target_pairs={{0,96},{32,0},{64,32},{96,64},{1,97},{33,1},{65,33},{97,65},{2,98}... | collective-permute-start | bytes 1572872 | tf_op jit(solution)/shard_map/ppermute | solution.py:349
  190.4 24.8 %collective-permute-start.18 = (bf16[4,4,128,128]{3,2,1,0:T(8,128)(2,1)S(1)}, bf16[4,4,128,128]{3,2,1,0:T(8,128)(2,1)S(1)}, u32[]{:S(2)}, u32[]{:S(2)}) collective-permute-start(bf16[4,4,128,128]{3,2,1,0:T(8,128)(2,1)S(1)} %add_convert_fusion.1), channel_id=1, source_target_pairs={{0,32},{32,64},{64,96},{96,0},{1,33},{33,65},{65,97},{97,1},{2,34}... | collective-permute-start | bytes 1572872 | tf_op jit(solution)/shard_map/ppermute | solution.py:349
  197.6 17.6 %copy-start.6 = (bf16[4,4,128,128]{3,2,1,0:T(8,128)(2,1)S(1)}, bf16[4,4,128,128]{3,2,1,0:T(8,128)(2,1)}, u32[]{:S(2)}) copy-start(bf16[4,4,128,128]{3,2,1,0:T(8,128)(2,1)} %get-tuple-element.43) | copy-start | bytes 1572868
  200.9 2.3 collective-permute-start.10
  203.2 4.6 %collective-permute-start.11 = (bf16[1,2,32,512]{3,2,1,0:T(8,128)(2,1)S(1)}, bf16[1,2,32,512]{3,2,1,0:T(8,128)(2,1)S(1)}, u32[]{:S(2)}, u32[]{:S(2)}) collective-permute-start(bf16[1,2,32,512]{3,2,1,0:T(8,128)(2,1)S(1)} %bitcast.41), channel_id=1, source_target_pairs={{0,7},{1,0},{2,1},{3,2},{4,3},{5,4},{6,5},{7,6},{8,15},{9,8},{10,9... | collective-permute-start | bytes 196616 | tf_op jit(solution)/shard_map/ppermute | solution.py:361
  208.8 7.9 %copy-start.9 = (bf16[4,2,32,512]{3,2,1,0:T(8,128)(2,1)}, bf16[4,2,32,512]{3,2,1,0:T(8,128)(2,1)S(1)}, u32[]{:S(2)}) copy-start(bf16[4,2,32,512]{3,2,1,0:T(8,128)(2,1)S(1)} %pad_maximum_fusion.2.own_ref) | copy-start | bytes 786436
  208.8 20.3 %collective-permute-start.12 = (bf16[4,2,32,512]{3,2,1,0:T(8,128)(2,1)S(1)}, bf16[4,2,32,512]{3,2,1,0:T(8,128)(2,1)}, u32[]{:S(2)}, u32[]{:S(2)}) collective-permute-start(bf16[4,2,32,512]{3,2,1,0:T(8,128)(2,1)S(1)} %pad_maximum_fusion.2.own_ref), channel_id=1, source_target_pairs={{0,8},{8,16},{16,24},{24,32},{32,40},{40,48},{48,56},{56,64},{64,7... | collective-permute-start | bytes 786440 | tf_op jit(solution)/shard_map/ppermute | solution.py:367
  217.7 27.7 %all-to-all-start.3 = ((bf16[128,24,128]{2,1,0:T(8,128)(2,1)}), bf16[128,24,128]{2,1,0:T(8,128)(2,1)S(1)}, u32[]{:S(2)}, u32[]{:S(2)}) async-start(bf16[128,24,128]{2,1,0:T(8,128)(2,1)} %pad_maximum_fusion), calls=%async_computation.3 | async-start | bytes 1572864 | tf_op jit(solution)/shard_map/all_to_all | solution.py:372
  (8 other events, 14.7 us)

commit v3 on v2

--- a/solution.py
+++ b/solution.py
@@ -54,7 +54,8 @@
 def write_rows(value, head, place, out_ref, stage_ref):
     for frame in range(2):
         stage_ref[head, pl.ds(frame, ROWS, stride=2), :] = value[frame * ROWS : (frame + 1) * ROWS]
-    out_ref[:, head, :, place] = stage_ref[head].reshape(4, 2, 8, 128).astype(BF)
+    value = stage_ref[head, : 2 * ROWS]
+    out_ref[:, head, :, place] = value.reshape(4, 2, 8, 128).astype(BF)
 
 
 def write_columns(tile_of, out_ref, stage_ref, place):
@@ -88,7 +89,7 @@
 
 def frame_rows(values, tile, stage_ref):
     for col in range(2):
-        stage_ref[2 * tile + col] = values[col]
+        stage_ref[2 * tile + col, : 2 * ROWS] = values[col]
     for frame in range(2):
         yield frame, [stage_ref[2 * tile + col, pl.ds(frame, ROWS, stride=2), :] for col in range(2)]
 
@@ -167,13 +168,15 @@
         write_columns(tile_of, out_ref, stage_ref, 0)
 
 
-def project_body(in_ref, proj_ref, out_ref, att_ref, stage_ref):
+def project_body(in_ref, proj_ref, first_ref, second_ref, att_ref, stage_ref):
     for tile in range(8):
         for frame, cols in frame_rows(heads_of(in_ref, tile, 0), tile, stage_ref):
             for col in range(2):
                 row = (col * 2 + frame) * ROWS
                 att_ref[row : row + ROWS, tile * 128 : (tile + 1) * 128] = cols[col].astype(BF)
-    out_ref[...] = dot(att_ref[...], proj_ref[...]).astype(BF)
+    out = dot(att_ref[...], proj_ref[...]).astype(BF)
+    first_ref[...] = out[: 2 * ROWS].reshape(first_ref.shape)
+    second_ref[...] = out[2 * ROWS :].reshape(second_ref.shape)
 
 
 def unpack_body(in_ref, gq_ref, gk_ref, gv_ref, stage_ref):
@@ -353,16 +356,16 @@
     return lax.ppermute(value, "c", [(0, 1), (1, 0)])
 
 
-def halo(own, forward):
+def halo(cols, forward):
     step = 1 if forward else -1
 
     def turn(value, cols):
         pairs = [(i, (i + cols) % 8) for i in range(8)]
         return lax.ppermute(value, ("z", "c"), pairs)
 
-    left = turn(own[1:], 1)
-    right = turn(own[:1], -1)
-    wide = jnp.concatenate([left, own, right], axis=0)
+    left = turn(cols[1], 1)
+    right = turn(cols[0], -1)
+    wide = jnp.stack([left, *cols, right])
     frames = [(t, t + step) for t in range(16) if 0 <= t + step < 16]
     return wide, lax.ppermute(wide, ("y", "x"), frames)
 
@@ -386,7 +389,7 @@
 
 def shards(queries, key_rows, value_rows, out_proj, conv_taps, cotangent):
     channels = out_proj.shape[1]
-    stage = pltpu.VMEM((16, 2 * ROWS, 128), F32)
+    stage = pltpu.VMEM((16, 2 * ROWS + 8, 128), F32)
     taps_spec = pl.BlockSpec((1, 1, 3, channels, channels), lambda t: (t // 3, t % 3, 0, 0, 0))
     conv_scratch = [
         pltpu.VMEM((3, 4, 4, ROWS, channels), BF),
@@ -394,7 +397,7 @@
     ]
     grouped = (4, 4, 128, 128)
 
-    near = halo(columns_first(cotangent), False)
+    near = halo(tuple(columns_first(cotangent)), False)
     (packed,) = kernel_call(
         pack_body,
         [struct((4, 16, 2, 3, 8, 128))],
@@ -477,14 +480,14 @@
         if not last:
             joined = shift_y(joined.astype(BF), 4 - steps).astype(F32)
         total = joined if total is None else total + joined
-    (projected,) = kernel_call(
+    projected = kernel_call(
         project_body,
-        [struct((4 * ROWS, channels))],
+        [struct((2, ROWS, channels))] * 2,
         [pltpu.VMEM((4 * ROWS, 1024), BF), stage],
         (att, out_proj),
         us=3.0,
     )
-    near = halo(projected.reshape(2, 2, ROWS, channels), True)
+    near = halo(projected, True)
     (conv,) = kernel_call(
         conv_body,
         [struct((4 * ROWS, channels))],
@@ -501,7 +504,7 @@
     grads = kernel_call(
         unpack_body,
         [struct((2 * ROWS, 2, 1024))] * 3,
-        [pltpu.VMEM((3, 16, 2 * ROWS, 128), F32)],
+        [pltpu.VMEM((3, 16, 2 * ROWS + 8, 128), F32)],
         (grads,),
         us=4.0,
     )

time: 251 us -> 251 us (level)
  transfers between devices with their start and end apart: 24 -> 24, of which waited for: 10 -> 10; matrix products, arithmetic and copies ran while one was open for 3% -> 2% of each run, Pallas kernels for 37% -> 37%
where the time goes in v3:
time: 251 us; the launch traced here: 250 us
  Pallas kernels  140 us (56%)
  starting transfers between devices  71.8 us (29%)
  waiting for transfers between devices  27.4 us (11%)
  local copies, waits for them, and re-layouts  6.46 us (3%)
  other arithmetic  3.85 us (2%)
    pallas_call x11, Pallas kernels, kernel_call(): pl.pallas_call(body, out_shape=outs, grid=grid, in_specs=in_specs, out_sp...  140 us
    all_to_all x4, starting transfers between devices, exchange_all(): return lax.all_to_all(split, AXES, split_axis=0, concat_axis=0, tiled=True)  34 us
    ppermute x8, starting transfers between devices, swap_core(): return lax.ppermute(value, 'c', [(0, 1), (1, 0)])  18.7 us
    all_to_all x4, waiting for transfers between devices, exchange_all(): return lax.all_to_all(split, AXES, split_axis=0, concat_axis=0, tiled=True)  13.2 us
    ppermute x6, waiting for transfers between devices, shift_y(): return lax.ppermute(value, 'y', [(i, (i + steps) % 4) for i in range(4)])  7.64 us
    ppermute x4, starting transfers between devices, turn(): return lax.ppermute(value, ('z', 'c'), pairs)  7.58 us
    ppermute x6, starting transfers between devices, shift_y(): return lax.ppermute(value, 'y', [(i, (i + steps) % 4) for i in range(4)])  7.29 us
    ppermute x4, waiting for transfers between devices, turn(): return lax.ppermute(value, ('z', 'c'), pairs)  6.45 us
  transfers between devices with their start and end apart: 24, of which 10 were waited for; matrix products, arithmetic and copies ran while one was open for 2% of the time, Pallas kernels for 37%

profile of v3, /device:TPU:1, one launch (start us, length us, event | category | flops | bytes accessed | tf_op | source)
XLA Modules:
  0.0 249.9 jit_solution(13477212383135409086)
XLA Ops:
  1.6 3.0 %collective-permute-start = (bf16[2,32,512]{2,1,0:T(8,128)(2,1)S(1)}, bf16[2,32,512]{2,1,0:T(8,128)(2,1)S(1)}, u32[]{:S(2)}, u32[]{:S(2)}) collective-permute-start(bf16[2,32,512]{2,1,0:T(8,128)(2,1)S(1)} %get-tuple-element.52), channel_id=1, source_target_pairs={{0,1},{1,2},{2,3},{3,4},{4,5},{5,6},{6,7},{7,0},{8,9},{9,10},{10,1... | collective-permute-start | bytes 196616 | tf_op jit(solution)/shard_map/ppermute | solution.py:364
  4.6 1.3 collective-permute-done
  5.9 2.4 collective-permute-done.1
  9.6 3.8 %shard_map.93 = bf16[4,16,2,3,8,128]{5,4,3,2,1,0:T(8,128)(2,1)} custom-call(bf16[64,2,1024]{2,1,0:T(2,128)(2,1)} %bitcast.53, bf16[64,2,1024]{2,1,0:T(2,128)(2,1)} %bitcast.54, bf16[64,2,1024]{2,1,0:T(2,128)(2,1)} %bitcast.55), custom_call_target="tpu_custom_call" | custom-call | flops 3200000000 | bytes 4000000 | tf_op jit(solution)/shard_map/pallas_call | solution.py:36
  13.5 10.6 %all-to-all-start = ((bf16[128,24,128]{2,1,0:T(8,128)(2,1)}), bf16[128,24,128]{2,1,0:T(8,128)(2,1)S(1)}, u32[]{:S(2)}, u32[]{:S(2)}) async-start(bf16[128,24,128]{2,1,0:T(8,128)(2,1)} %bitcast.35), calls=%async_computation | async-start | bytes 1572864 | tf_op jit(solution)/shard_map/all_to_all | solution.py:375
  24.7 12.4 %shard_map.94 = bf16[4,16,2,1,8,128]{5,4,3,2,1,0:T(8,128)(2,1)} custom-call(bf16[4,2,32,512]{3,2,1,0:T(8,128)(2,1)} %copy-done.10, bf16[4,2,32,512]{3,2,1,0:T(8,128)(2,1)} %copy-done.15, bf16[3,3,3,512,512]{4,3,2,1,0:T(8,128)(2,1)} %taps_ref.3, bf16[1024,512]{1,0:T(8,128)(2,1)} %proj_ref.3), custom_call_target="tpu_custom_call" | custom-call | flops 9600000000 | bytes 12000000 | tf_op jit(solution)/shard_map/pallas_call | solution.py:36
  37.2 3.1 %all-to-all-done.refs_2_ = bf16[128,24,128]{2,1,0:T(8,128)(2,1)S(1)} async-done(((bf16[128,24,128]{2,1,0:T(8,128)(2,1)}), bf16[128,24,128]{2,1,0:T(8,128)(2,1)S(1)}, u32[]{:S(2)}, u32[]{:S(2)}) %all-to-all-start) | async-done | bytes 786464 | tf_op jit(solution)/shard_map/all_to_all | solution.py:375
  40.7 2.3 collective-permute-start.4
  43.1 1.9 collective-permute-start.9
  44.9 5.9 %all-to-all-start.1 = ((bf16[128,8,128]{2,1,0:T(8,128)(2,1)}), bf16[128,8,128]{2,1,0:T(8,128)(2,1)S(1)}, u32[]{:S(2)}, u32[]{:S(2)}) async-start(bf16[128,8,128]{2,1,0:T(8,128)(2,1)} %bitcast.42), calls=%async_computation.1 | async-start | bytes 524288 | tf_op jit(solution)/shard_map/all_to_all | solution.py:375
  50.9 3.6 %collective-permute-done.3.refs_0_.same_ref = bf16[4,4,128,128]{3,2,1,0:T(8,128)(2,1)S(1)} collective-permute-done((bf16[4,4,128,128]{3,2,1,0:T(8,128)(2,1)S(1)}, bf16[4,4,128,128]{3,2,1,0:T(8,128)(2,1)S(1)}, u32[]{:S(2)}, u32[]{:S(2)}) %collective-permute-start.3) | collective-permute-done | bytes 524320 | tf_op jit(solution)/shard_map/ppermute | solution.py:352
  54.5 15.3 %collective-permute-start.6 = (bf16[4,4,128,128]{3,2,1,0:T(8,128)(2,1)S(1)}, bf16[4,4,128,128]{3,2,1,0:T(8,128)(2,1)}, u32[]{:S(2)}, u32[]{:S(2)}) collective-permute-start(bf16[4,4,128,128]{3,2,1,0:T(8,128)(2,1)S(1)} %collective-permute-done.3.refs_0_.same_ref), channel_id=1, source_target_pairs={{0,1},{1,0},{2,3},{3,2},{4,5},{5,4},{6,7},{7,6},{8,9},{9,8},{10,11... | collective-permute-start | bytes 1572872 | tf_op jit(solution)/shard_map/ppermute | solution.py:356
  71.1 11.3 %shard_map.95 = (bf16[2048,128]{1,0:T(8,128)(2,1)}, f32[2048,128]{1,0:T(8,128)}) custom-call(bf16[4,4,128,128]{3,2,1,0:T(8,128)(2,1)} %bitcast.40, bf16[4,4,128,128]{3,2,1,0:T(8,128)(2,1)} %copy-done.12, bf16[128,24,128]{2,1,0:T(8,128)(2,1)} %copy-done), custom_call_target="tpu_custom_call" | custom-call | flops 8000000000 | bytes 10000000 | tf_op jit(solution)/shard_map/pallas_call | solution.py:36
  83.2 25.7 %shard_map.96 = (bf16[1024,128]{1,0:T(8,128)(2,1)}, f32[8,2048]{1,0:T(8,128)}, bf16[2048,128]{1,0:T(8,128)(2,1)}) custom-call(bf16[4,4,128,128]{3,2,1,0:T(8,128)(2,1)} %copy-done.14, bf16[4,4,128,128]{3,2,1,0:T(8,128)(2,1)} %copy-done.13, bf16[4,4,128,128]{3,2,1,0:T(8,128)(2,1)} %collective-permute-done.5.refs_2_.same_ref, ...), custom_call_target="tpu_custom_call" | custom-call | flops 20000000000 | bytes 25000000 | tf_op jit(solution)/shard_map/pallas_call | solution.py:36
  108.9 17.2 %shard_map.99 = (bf16[4,4,128,128]{3,2,1,0:T(8,128)(2,1)}, bf16[4,4,128,128]{3,2,1,0:T(8,128)(2,1)}, f32[128,2048]{1,0:T(8,128)}) custom-call(bf16[4,4,128,128]{3,2,1,0:T(8,128)(2,1)} %collective-permute-done.5.refs_2_.same_ref, bf16[4,4,128,128]{3,2,1,0:T(8,128)(2,1)} %collective-permute-done.8.refs_5_.other_ref, ...), custom_call_target="tpu_custom_call" | custom-call | flops 12800000000 | bytes 16000000 | tf_op jit(solution)/shard_map/pallas_call | solution.py:36
  126.5 17.6 %shard_map.100 = (bf16[4,4,128,128]{3,2,1,0:T(8,128)(2,1)}, bf16[4,4,128,128]{3,2,1,0:T(8,128)(2,1)}, f32[128,2048]{1,0:T(8,128)}) custom-call(bf16[4,4,128,128]{3,2,1,0:T(8,128)(2,1)} %copy-done.14, bf16[4,4,128,128]{3,2,1,0:T(8,128)(2,1)} %collective-permute-done.6.refs_3_.other_ref, bf16[2048,128]{1,0:T(8,128)(2,1)} %get-tuple-element.29.refs_6_.query_ref, ...), custom_call_target="tpu_custom_call" | custom-call | flops 12800000000 | bytes 16000000 | tf_op jit(solution)/shard_map/pallas_call | solution.py:36
  144.3 17.7 %shard_map.101 = (bf16[4,4,128,128]{3,2,1,0:T(8,128)(2,1)}, bf16[4,4,128,128]{3,2,1,0:T(8,128)(2,1)}, f32[128,2048]{1,0:T(8,128)}) custom-call(bf16[4,4,128,128]{3,2,1,0:T(8,128)(2,1)} %copy-done.13, bf16[4,4,128,128]{3,2,1,0:T(8,128)(2,1)} %collective-permute-done.7.refs_4_.other_ref, bf16[2048,128]{1,0:T(8,128)(2,1)} %get-tuple-element.29.refs_6_.query_ref, ...), custom_call_target="tpu_custom_call" | custom-call | flops 12800000000 | bytes 16000000 | tf_op jit(solution)/shard_map/pallas_call | solution.py:36
  162.3 17.4 %shard_map.102 = (bf16[4,4,128,128]{3,2,1,0:T(8,128)(2,1)}, bf16[4,4,128,128]{3,2,1,0:T(8,128)(2,1)}, bf16[1024,128]{1,0:T(8,128)(2,1)}) custom-call(bf16[4,4,128,128]{3,2,1,0:T(8,128)(2,1)} %bitcast.41, bf16[4,4,128,128]{3,2,1,0:T(8,128)(2,1)} %copy-done.12, bf16[2048,128]{1,0:T(8,128)(2,1)} %get-tuple-element.29.refs_6_.query_ref, ...), custom_call_target="tpu_custom_call" | custom-call | flops 12800000000 | bytes 16000000 | tf_op jit(solution)/shard_map/pallas_call | solution.py:36
  179.9 6.1 %all-to-all-start.2 = ((bf16[128,8,128]{2,1,0:T(8,128)(2,1)}), bf16[128,8,128]{2,1,0:T(8,128)(2,1)S(1)}, u32[]{:S(2)}, u32[]{:S(2)}) async-start(bf16[128,8,128]{2,1,0:T(8,128)(2,1)} %bitcast.11), calls=%async_computation.2 | async-start | bytes 524288 | tf_op jit(solution)/shard_map/all_to_all | solution.py:375
  186.2 2.9 %collective-permute-start.14 = (bf16[4,4,128,128]{3,2,1,0:T(8,128)(2,1)S(1)}, bf16[4,4,128,128]{3,2,1,0:T(8,128)(2,1)S(1)}, u32[]{:S(2)}, u32[]{:S(2)}) collective-permute-start(bf16[4,4,128,128]{3,2,1,0:T(8,128)(2,1)S(1)} %add_convert_fusion.3), channel_id=1, source_target_pairs={{0,64},{32,96},{64,0},{96,32},{1,65},{33,97},{65,1},{97,33},{2,66}... | collective-permute-start | bytes 1572872 | tf_op jit(solution)/shard_map/ppermute | solution.py:352
  191.1 5.9 %all-to-all-done.2 = bf16[128,8,128]{2,1,0:T(8,128)(2,1)S(1)} async-done(((bf16[128,8,128]{2,1,0:T(8,128)(2,1)}), bf16[128,8,128]{2,1,0:T(8,128)(2,1)S(1)}, u32[]{:S(2)}, u32[]{:S(2)}) %all-to-all-start.2) | async-done | bytes 262176 | tf_op jit(solution)/shard_map/all_to_all | solution.py:375
  197.6 2.4 shard_map.97
  201.0 1.6 collective-permute-done.10
  202.6 3.6 %collective-permute-start.11 = (bf16[2,32,512]{2,1,0:T(8,128)(2,1)}, bf16[2,32,512]{2,1,0:T(8,128)(2,1)S(1)}, u32[]{:S(2)}, u32[]{:S(2)}) collective-permute-start(bf16[2,32,512]{2,1,0:T(8,128)(2,1)} %get-tuple-element.34), channel_id=1, source_target_pairs={{0,7},{1,0},{2,1},{3,2},{4,3},{5,4},{6,5},{7,6},{8,15},{9,8},{10,9... | collective-permute-start | bytes 196616 | tf_op jit(solution)/shard_map/ppermute | solution.py:364
  208.3 2.9 %collective-permute-start.12 = (bf16[4,2,32,512]{3,2,1,0:T(8,128)(2,1)S(1)}, bf16[4,2,32,512]{3,2,1,0:T(8,128)(2,1)}, u32[]{:S(2)}, u32[]{:S(2)}) collective-permute-start(bf16[4,2,32,512]{3,2,1,0:T(8,128)(2,1)S(1)} %pad_maximum_fusion.2.own_ref), channel_id=1, source_target_pairs={{0,8},{8,16},{16,24},{24,32},{32,40},{40,48},{48,56},{56,64},{64,7... | collective-permute-start | bytes 786440 | tf_op jit(solution)/shard_map/ppermute | solution.py:370
  211.2 3.1 %collective-permute-done.16 = bf16[4,4,128,128]{3,2,1,0:T(8,128)(2,1)S(1)} collective-permute-done((bf16[4,4,128,128]{3,2,1,0:T(8,128)(2,1)S(1)}, bf16[4,4,128,128]{3,2,1,0:T(8,128)(2,1)S(1)}, u32[]{:S(2)}, u32[]{:S(2)}) %collective-permute-start.16) | collective-permute-done | bytes 524320 | tf_op jit(solution)/shard_map/ppermute | solution.py:352
  215.2 1.5 add_convert_fusion
  217.7 11.4 %all-to-all-start.3 = ((bf16[128,24,128]{2,1,0:T(8,128)(2,1)}), bf16[128,24,128]{2,1,0:T(8,128)(2,1)S(1)}, u32[]{:S(2)}, u32[]{:S(2)}) async-start(bf16[128,24,128]{2,1,0:T(8,128)(2,1)} %pad_maximum_fusion), calls=%async_computation.3 | async-start | bytes 1572864 | tf_op jit(solution)/shard_map/all_to_all | solution.py:375
  229.1 10.2 %shard_map.98 = bf16[128,512]{1,0:T(8,128)(2,1)} custom-call(bf16[4,2,32,512]{3,2,1,0:T(8,128)(2,1)} %copy-done.9, bf16[4,2,32,512]{3,2,1,0:T(8,128)(2,1)} %collective-permute-done.12.near_ref, bf16[3,3,3,512,512]{4,3,2,1,0:T(8,128)(2,1)} %taps_ref.3), custom_call_target="tpu_custom_call" | custom-call | flops 8000000000 | bytes 10000000 | tf_op jit(solution)/shard_map/pallas_call | solution.py:36
  239.4 1.7 copy.14
  241.1 4.3 %all-to-all-done.3 = bf16[128,24,128]{2,1,0:T(8,128)(2,1)S(1)} async-done(((bf16[128,24,128]{2,1,0:T(8,128)(2,1)}), bf16[128,24,128]{2,1,0:T(8,128)(2,1)S(1)}, u32[]{:S(2)}, u32[]{:S(2)}) %all-to-all-start.3) | async-done | bytes 786464 | tf_op jit(solution)/shard_map/all_to_all | solution.py:375
  246.3 3.7 %shard_map.103 = (bf16[64,2,1024]{2,1,0:T(2,128)(2,1)}, bf16[64,2,1024]{2,1,0:T(2,128)(2,1)}, bf16[64,2,1024]{2,1,0:T(2,128)(2,1)}) custom-call(bf16[4,16,2,3,8,128]{5,4,3,2,1,0:T(8,128)(2,1)} %bitcast.34), custom_call_target="tpu_custom_call" | custom-call | flops 3200000000 | bytes 4000000 | tf_op jit(solution)/shard_map/pallas_call | solution.py:36
  (70 shorter events, 14.9 us)
Async XLA Ops:
  1.6 4.4 %collective-permute-start = (bf16[2,32,512]{2,1,0:T(8,128)(2,1)S(1)}, bf16[2,32,512]{2,1,0:T(8,128)(2,1)S(1)}, u32[]{:S(2)}, u32[]{:S(2)}) collective-permute-start(bf16[2,32,512]{2,1,0:T(8,128)(2,1)S(1)} %get-tuple-element.52), channel_id=1, source_target_pairs={{0,1},{1,2},{2,3},{3,4},{4,5},{5,6},{6,7},{7,0},{8,9},{9,10},{10,1... | collective-permute-start | bytes 196616 | tf_op jit(solution)/shard_map/ppermute | solution.py:364
  4.6 3.7 %collective-permute-start.1 = (bf16[2,32,512]{2,1,0:T(8,128)(2,1)S(1)}, bf16[2,32,512]{2,1,0:T(8,128)(2,1)S(1)}, u32[]{:S(2)}, u32[]{:S(2)}) collective-permute-start(bf16[2,32,512]{2,1,0:T(8,128)(2,1)S(1)} %get-tuple-element.53), channel_id=1, source_target_pairs={{0,7},{1,0},{2,1},{3,2},{4,3},{5,4},{6,5},{7,6},{8,15},{9,8},{10,9... | collective-permute-start | bytes 196616 | tf_op jit(solution)/shard_map/ppermute | solution.py:364
  8.3 15.7 %collective-permute-start.2 = (bf16[4,2,32,512]{3,2,1,0:T(8,128)(2,1)S(1)}, bf16[4,2,32,512]{3,2,1,0:T(8,128)(2,1)S(1)}, u32[]{:S(2)}, u32[]{:S(2)}) collective-permute-start(bf16[4,2,32,512]{3,2,1,0:T(8,128)(2,1)S(1)} %pad_maximum_fusion.1.own_ref), channel_id=1, source_target_pairs={{8,0},{16,8},{24,16},{32,24},{40,32},{48,40},{56,48},{64,56},{72,6... | collective-permute-start | bytes 786440 | tf_op jit(solution)/shard_map/ppermute | solution.py:370
  13.5 26.8 %all-to-all-start = ((bf16[128,24,128]{2,1,0:T(8,128)(2,1)}), bf16[128,24,128]{2,1,0:T(8,128)(2,1)S(1)}, u32[]{:S(2)}, u32[]{:S(2)}) async-start(bf16[128,24,128]{2,1,0:T(8,128)(2,1)} %bitcast.35), calls=%async_computation | async-start | bytes 1572864 | tf_op jit(solution)/shard_map/all_to_all | solution.py:375
  40.3 30.1 %copy-start = (bf16[128,24,128]{2,1,0:T(8,128)(2,1)}, bf16[128,24,128]{2,1,0:T(8,128)(2,1)S(1)}, u32[]{:S(2)}) copy-start(bf16[128,24,128]{2,1,0:T(8,128)(2,1)S(1)} %all-to-all-done.refs_2_) | copy-start | bytes 2359300
  40.3 30.0 %copy-start.5 = (bf16[128,16,128]{2,1,0:T(8,128)(2,1)}, bf16[128,16,128]{2,1,0:T(8,128)(2,1)S(1)}, u32[]{:S(2)}) copy-start(bf16[128,16,128]{2,1,0:T(8,128)(2,1)S(1)} %slice.4) | copy-start | bytes 1572868
  40.3 14.2 %collective-permute-start.3 = (bf16[4,4,128,128]{3,2,1,0:T(8,128)(2,1)S(1)}, bf16[4,4,128,128]{3,2,1,0:T(8,128)(2,1)S(1)}, u32[]{:S(2)}, u32[]{:S(2)}) collective-permute-start(bf16[4,4,128,128]{3,2,1,0:T(8,128)(2,1)S(1)} %bitcast.36), channel_id=1, source_target_pairs={{0,32},{32,64},{64,96},{96,0},{1,33},{33,65},{65,97},{97,1},{2,34}... | collective-permute-start | bytes 1572872 | tf_op jit(solution)/shard_map/ppermute | solution.py:352
  40.7 29.1 %collective-permute-start.4 = (bf16[4,4,128,128]{3,2,1,0:T(8,128)(2,1)S(1)}, bf16[4,4,128,128]{3,2,1,0:T(8,128)(2,1)S(1)}, u32[]{:S(2)}, u32[]{:S(2)}) collective-permute-start(bf16[4,4,128,128]{3,2,1,0:T(8,128)(2,1)S(1)} %bitcast.37), channel_id=1, source_target_pairs={{0,96},{32,0},{64,32},{96,64},{1,97},{33,1},{65,33},{97,65},{2,98}... | collective-permute-start | bytes 1572872 | tf_op jit(solution)/shard_map/ppermute | solution.py:352
  43.1 26.8 %collective-permute-start.5 = (bf16[4,4,128,128]{3,2,1,0:T(8,128)(2,1)S(1)}, bf16[4,4,128,128]{3,2,1,0:T(8,128)(2,1)}, u32[]{:S(2)}, u32[]{:S(2)}) collective-permute-start(bf16[4,4,128,128]{3,2,1,0:T(8,128)(2,1)S(1)} %bitcast.38), channel_id=1, source_target_pairs={{0,64},{32,96},{64,0},{96,32},{1,65},{33,97},{65,1},{97,33},{2,66}... | collective-permute-start | bytes 1572872 | tf_op jit(solution)/shard_map/ppermute | solution.py:352
  43.1 27.3 %collective-permute-start.9 = (bf16[4,4,128,128]{3,2,1,0:T(8,128)(2,1)S(1)}, bf16[4,4,128,128]{3,2,1,0:T(8,128)(2,1)S(1)}, u32[]{:S(2)}, u32[]{:S(2)}) collective-permute-start(bf16[4,4,128,128]{3,2,1,0:T(8,128)(2,1)S(1)} %bitcast.39), channel_id=1, source_target_pairs={{0,1},{1,0},{2,3},{3,2},{4,5},{5,4},{6,7},{7,6},{8,9},{9,8},{10,11... | collective-permute-start | bytes 1572872 | tf_op jit(solution)/shard_map/ppermute | solution.py:356
  44.9 37.5 %all-to-all-start.1 = ((bf16[128,8,128]{2,1,0:T(8,128)(2,1)}), bf16[128,8,128]{2,1,0:T(8,128)(2,1)S(1)}, u32[]{:S(2)}, u32[]{:S(2)}) async-start(bf16[128,8,128]{2,1,0:T(8,128)(2,1)} %bitcast.42), calls=%async_computation.1 | async-start | bytes 524288 | tf_op jit(solution)/shard_map/all_to_all | solution.py:375
  54.5 28.0 %copy-start.14 = (bf16[4,4,128,128]{3,2,1,0:T(8,128)(2,1)}, bf16[4,4,128,128]{3,2,1,0:T(8,128)(2,1)S(1)}, u32[]{:S(2)}) copy-start(bf16[4,4,128,128]{3,2,1,0:T(8,128)(2,1)S(1)} %collective-permute-done.3.refs_0_.same_ref) | copy-start | bytes 1572868
  54.5 28.0 %collective-permute-start.6 = (bf16[4,4,128,128]{3,2,1,0:T(8,128)(2,1)S(1)}, bf16[4,4,128,128]{3,2,1,0:T(8,128)(2,1)}, u32[]{:S(2)}, u32[]{:S(2)}) collective-permute-start(bf16[4,4,128,128]{3,2,1,0:T(8,128)(2,1)S(1)} %collective-permute-done.3.refs_0_.same_ref), channel_id=1, source_target_pairs={{0,1},{1,0},{2,3},{3,2},{4,5},{5,4},{6,7},{7,6},{8,9},{9,8},{10,11... | collective-permute-start | bytes 1572872 | tf_op jit(solution)/shard_map/ppermute | solution.py:356
  69.8 12.7 %copy-start.13 = (bf16[4,4,128,128]{3,2,1,0:T(8,128)(2,1)}, bf16[4,4,128,128]{3,2,1,0:T(8,128)(2,1)S(1)}, u32[]{:S(2)}) copy-start(bf16[4,4,128,128]{3,2,1,0:T(8,128)(2,1)S(1)} %collective-permute-done.4.refs_1_.same_ref) | copy-start | bytes 1572868
  69.8 12.7 %collective-permute-start.7 = (bf16[4,4,128,128]{3,2,1,0:T(8,128)(2,1)S(1)}, bf16[4,4,128,128]{3,2,1,0:T(8,128)(2,1)}, u32[]{:S(2)}, u32[]{:S(2)}) collective-permute-start(bf16[4,4,128,128]{3,2,1,0:T(8,128)(2,1)S(1)} %collective-permute-done.4.refs_1_.same_ref), channel_id=1, source_target_pairs={{0,1},{1,0},{2,3},{3,2},{4,5},{5,4},{6,7},{7,6},{8,9},{9,8},{10,11... | collective-permute-start | bytes 1572872 | tf_op jit(solution)/shard_map/ppermute | solution.py:356
  69.9 12.6 %collective-permute-start.8 = (bf16[4,4,128,128]{3,2,1,0:T(8,128)(2,1)}, bf16[4,4,128,128]{3,2,1,0:T(8,128)(2,1)}, u32[]{:S(2)}, u32[]{:S(2)}) collective-permute-start(bf16[4,4,128,128]{3,2,1,0:T(8,128)(2,1)} %collective-permute-done.5.refs_2_.same_ref), channel_id=1, source_target_pairs={{0,1},{1,0},{2,3},{3,2},{4,5},{5,4},{6,7},{7,6},{8,9},{9,8},{10,11... | collective-permute-start | bytes 1572872 | tf_op jit(solution)/shard_map/ppermute | solution.py:356
  126.2 59.9 %collective-permute-start.13 = (bf16[4,4,128,128]{3,2,1,0:T(8,128)(2,1)}, bf16[4,4,128,128]{3,2,1,0:T(8,128)(2,1)S(1)}, u32[]{:S(2)}, u32[]{:S(2)}) collective-permute-start(bf16[4,4,128,128]{3,2,1,0:T(8,128)(2,1)} %get-tuple-element.42), channel_id=1, source_target_pairs={{0,1},{1,0},{2,3},{3,2},{4,5},{5,4},{6,7},{7,6},{8,9},{9,8},{10,11... | collective-permute-start | bytes 1572872 | tf_op jit(solution)/shard_map/ppermute | solution.py:356
  144.1 45.1 %collective-permute-start.15 = (bf16[4,4,128,128]{3,2,1,0:T(8,128)(2,1)}, bf16[4,4,128,128]{3,2,1,0:T(8,128)(2,1)S(1)}, u32[]{:S(2)}, u32[]{:S(2)}) collective-permute-start(bf16[4,4,128,128]{3,2,1,0:T(8,128)(2,1)} %get-tuple-element.44), channel_id=1, source_target_pairs={{0,1},{1,0},{2,3},{3,2},{4,5},{5,4},{6,7},{7,6},{8,9},{9,8},{10,11... | collective-permute-start | bytes 1572872 | tf_op jit(solution)/shard_map/ppermute | solution.py:356
  162.0 28.3 %collective-permute-start.17 = (bf16[4,4,128,128]{3,2,1,0:T(8,128)(2,1)}, bf16[4,4,128,128]{3,2,1,0:T(8,128)(2,1)S(1)}, u32[]{:S(2)}, u32[]{:S(2)}) collective-permute-start(bf16[4,4,128,128]{3,2,1,0:T(8,128)(2,1)} %get-tuple-element.46), channel_id=1, source_target_pairs={{0,1},{1,0},{2,3},{3,2},{4,5},{5,4},{6,7},{7,6},{8,9},{9,8},{10,11... | collective-permute-start | bytes 1572872 | tf_op jit(solution)/shard_map/ppermute | solution.py:356
  162.3 23.8 %copy-start.4 = (bf16[4,4,128,128]{3,2,1,0:T(8,128)(2,1)S(1)}, bf16[4,4,128,128]{3,2,1,0:T(8,128)(2,1)}, u32[]{:S(2)}) copy-start(bf16[4,4,128,128]{3,2,1,0:T(8,128)(2,1)} %get-tuple-element.41) | copy-start | bytes 1572868
  179.7 9.5 %copy-start.3 = (bf16[4,4,128,128]{3,2,1,0:T(8,128)(2,1)S(1)}, bf16[4,4,128,128]{3,2,1,0:T(8,128)(2,1)}, u32[]{:S(2)}) copy-start(bf16[4,4,128,128]{3,2,1,0:T(8,128)(2,1)} %get-tuple-element.43) | copy-start | bytes 1572868
  179.7 31.5 %collective-permute-start.19 = (bf16[4,4,128,128]{3,2,1,0:T(8,128)(2,1)}, bf16[4,4,128,128]{3,2,1,0:T(8,128)(2,1)}, u32[]{:S(2)}, u32[]{:S(2)}) collective-permute-start(bf16[4,4,128,128]{3,2,1,0:T(8,128)(2,1)} %get-tuple-element.48), channel_id=1, source_target_pairs={{0,1},{1,0},{2,3},{3,2},{4,5},{5,4},{6,7},{7,6},{8,9},{9,8},{10,11... | collective-permute-start | bytes 1572872 | tf_op jit(solution)/shard_map/ppermute | solution.py:356
  179.9 17.0 %all-to-all-start.2 = ((bf16[128,8,128]{2,1,0:T(8,128)(2,1)}), bf16[128,8,128]{2,1,0:T(8,128)(2,1)S(1)}, u32[]{:S(2)}, u32[]{:S(2)}) async-start(bf16[128,8,128]{2,1,0:T(8,128)(2,1)} %bitcast.11), calls=%async_computation.2 | async-start | bytes 524288 | tf_op jit(solution)/shard_map/all_to_all | solution.py:375
  186.2 25.0 %collective-permute-start.14 = (bf16[4,4,128,128]{3,2,1,0:T(8,128)(2,1)S(1)}, bf16[4,4,128,128]{3,2,1,0:T(8,128)(2,1)S(1)}, u32[]{:S(2)}, u32[]{:S(2)}) collective-permute-start(bf16[4,4,128,128]{3,2,1,0:T(8,128)(2,1)S(1)} %add_convert_fusion.3), channel_id=1, source_target_pairs={{0,64},{32,96},{64,0},{96,32},{1,65},{33,97},{65,1},{97,33},{2,66}... | collective-permute-start | bytes 1572872 | tf_op jit(solution)/shard_map/ppermute | solution.py:352
  189.3 25.0 %collective-permute-start.16 = (bf16[4,4,128,128]{3,2,1,0:T(8,128)(2,1)S(1)}, bf16[4,4,128,128]{3,2,1,0:T(8,128)(2,1)S(1)}, u32[]{:S(2)}, u32[]{:S(2)}) collective-permute-start(bf16[4,4,128,128]{3,2,1,0:T(8,128)(2,1)S(1)} %add_convert_fusion.2), channel_id=1, source_target_pairs={{0,96},{32,0},{64,32},{96,64},{1,97},{33,1},{65,33},{97,65},{2,98}... | collective-permute-start | bytes 1572872 | tf_op jit(solution)/shard_map/ppermute | solution.py:352
  190.4 24.8 %collective-permute-start.18 = (bf16[4,4,128,128]{3,2,1,0:T(8,128)(2,1)S(1)}, bf16[4,4,128,128]{3,2,1,0:T(8,128)(2,1)S(1)}, u32[]{:S(2)}, u32[]{:S(2)}) collective-permute-start(bf16[4,4,128,128]{3,2,1,0:T(8,128)(2,1)S(1)} %add_convert_fusion.1), channel_id=1, source_target_pairs={{0,32},{32,64},{64,96},{96,0},{1,33},{33,65},{65,97},{97,1},{2,34}... | collective-permute-start | bytes 1572872 | tf_op jit(solution)/shard_map/ppermute | solution.py:352
  197.6 17.6 %copy-start.6 = (bf16[4,4,128,128]{3,2,1,0:T(8,128)(2,1)S(1)}, bf16[4,4,128,128]{3,2,1,0:T(8,128)(2,1)}, u32[]{:S(2)}) copy-start(bf16[4,4,128,128]{3,2,1,0:T(8,128)(2,1)} %get-tuple-element.47) | copy-start | bytes 1572868
  200.0 2.6 %collective-permute-start.10 = (bf16[2,32,512]{2,1,0:T(8,128)(2,1)}, bf16[2,32,512]{2,1,0:T(8,128)(2,1)S(1)}, u32[]{:S(2)}, u32[]{:S(2)}) collective-permute-start(bf16[2,32,512]{2,1,0:T(8,128)(2,1)} %get-tuple-element.33), channel_id=1, source_target_pairs={{0,1},{1,2},{2,3},{3,4},{4,5},{5,6},{6,7},{7,0},{8,9},{9,10},{10,1... | collective-permute-start | bytes 196616 | tf_op jit(solution)/shard_map/ppermute | solution.py:364
  202.6 4.7 %collective-permute-start.11 = (bf16[2,32,512]{2,1,0:T(8,128)(2,1)}, bf16[2,32,512]{2,1,0:T(8,128)(2,1)S(1)}, u32[]{:S(2)}, u32[]{:S(2)}) collective-permute-start(bf16[2,32,512]{2,1,0:T(8,128)(2,1)} %get-tuple-element.34), channel_id=1, source_target_pairs={{0,7},{1,0},{2,1},{3,2},{4,3},{5,4},{6,5},{7,6},{8,15},{9,8},{10,9... | collective-permute-start | bytes 196616 | tf_op jit(solution)/shard_map/ppermute | solution.py:364
  208.2 8.5 %copy-start.9 = (bf16[4,2,32,512]{3,2,1,0:T(8,128)(2,1)}, bf16[4,2,32,512]{3,2,1,0:T(8,128)(2,1)S(1)}, u32[]{:S(2)}) copy-start(bf16[4,2,32,512]{3,2,1,0:T(8,128)(2,1)S(1)} %pad_maximum_fusion.2.own_ref) | copy-start | bytes 786436
  208.3 20.9 %collective-permute-start.12 = (bf16[4,2,32,512]{3,2,1,0:T(8,128)(2,1)S(1)}, bf16[4,2,32,512]{3,2,1,0:T(8,128)(2,1)}, u32[]{:S(2)}, u32[]{:S(2)}) collective-permute-start(bf16[4,2,32,512]{3,2,1,0:T(8,128)(2,1)S(1)} %pad_maximum_fusion.2.own_ref), channel_id=1, source_target_pairs={{0,8},{8,16},{16,24},{24,32},{32,40},{40,48},{48,56},{56,64},{64,7... | collective-permute-start | bytes 786440 | tf_op jit(solution)/shard_map/ppermute | solution.py:370
  217.7 27.7 %all-to-all-start.3 = ((bf16[128,24,128]{2,1,0:T(8,128)(2,1)}), bf16[128,24,128]{2,1,0:T(8,128)(2,1)S(1)}, u32[]{:S(2)}, u32[]{:S(2)}) async-start(bf16[128,24,128]{2,1,0:T(8,128)(2,1)} %pad_maximum_fusion), calls=%async_computation.3 | async-start | bytes 1572864 | tf_op jit(solution)/shard_map/all_to_all | solution.py:375
  (8 other events, 14.7 us)
